TPU v7x, 32 devices: a whole 2x2x4 slice. The times are simulated.
32 devices in a mesh: fsdp: 4 (over z), emb: 8 (over y, x, core).
Axes of the slice: x: 2, y: 2, z: 4, core: 2. Of those that a mesh axis runs over, the one named last changes fastest.
Arguments:
- item_table: float32 [131072, 256], P(('fsdp', 'emb')), may hold values from -6 to 6
- item_owner: int32 [32, 1024, 1], P(('fsdp', 'emb')), may hold values from 0 to 31; in each aligned block of 1024 rows (0 to 1023, 1024 to 2047, ..., all dimensions but the last counted through in order) at most 64 rows name the same one
- item_row: int32 [32, 1024], P(('fsdp', 'emb')), may hold values from 0 to 4095
- staleness: int32 [131072], P(('fsdp', 'emb')), may hold values from 0 to 3
- w_proj: bfloat16 [2, 256, 1024], P(None, 'fsdp'), may hold values from -0.375 to 0.375
- w_out: bfloat16 [2, 256, 256], P(None, 'fsdp'), may hold values from -0.375 to 0.375
- out_grad: bfloat16 [32, 1024, 256], P(('fsdp', 'emb')), may hold values from -6 to 6
Outputs:
- new_table: float32 [131072, 256], P(('fsdp', 'emb'))
- w_proj_grad: float32 [2, 256, 1024], P(None, 'fsdp')
- w_out_grad: float32 [2, 256, 256], P(None, 'fsdp')
Inputs may be any that keep to these rules, and one draw needn't show every extreme that they name: `item_owner`: in each user's history no owner is named more than 64 times, a bound that some block reaches in every draw.
All inputs are finite; a program needn't handle non-finite values.
Results may differ from a plain program's by a relative error of at most 0.023.
Values may be sent and summed in bfloat16 or wider, within the bound.
No kernel may reach another device: no remote copies, remote signals or barrier semaphores. Data moves between devices by JAX's collectives and lax.ppermute only.
A program may use at most 128 MiB of HBM per device.

v0:
```python
import functools

import jax
import jax.numpy as jnp
from jax import lax
from jax.experimental import pallas as pl
from jax.experimental.pallas import tpu as pltpu
from jax.sharding import PartitionSpec as P

DH = 64
EPSILON = 1e-05
F32 = jnp.float32
BF16 = jnp.bfloat16


def nt_dot(a, b):
    return lax.dot_general(a, b, (((1,), (1,)), ((), ())), preferred_element_type=F32)


def nn_dot(a, b):
    return jnp.dot(a, b, preferred_element_type=F32)


def as_column(row):
    side = row.shape[1]
    same = lax.broadcasted_iota(jnp.int32, (side, side), 0) == lax.broadcasted_iota(
        jnp.int32, (side, side), 1
    )
    return jnp.sum(jnp.where(same, row.astype(F32), 0.0), axis=1, keepdims=True)


def index_kernel(owner_ref, row_ref, target_ref, request_ref):
    owners, capacity = request_ref.shape
    length = owner_ref.shape[1]
    lane = 128
    owner = owner_ref[...]
    member = (lax.broadcasted_iota(jnp.int32, (owners, length), 0) == owner).astype(F32)
    blocks = [member[:, at : at + lane] for at in range(0, length, lane)]
    stacked = jnp.concatenate(blocks, axis=0).astype(BF16)
    upper = (
        lax.broadcasted_iota(jnp.int32, (lane, lane), 0)
        < lax.broadcasted_iota(jnp.int32, (lane, lane), 1)
    ).astype(F32).astype(BF16)
    inside = nn_dot(stacked, upper)
    base = jnp.zeros((owners, 1), F32)
    slots = []
    for at, block in enumerate(blocks):
        earlier = inside[at * owners : (at + 1) * owners] + base
        slots.append(jnp.sum(earlier * block, axis=0, keepdims=True))
        base = base + jnp.sum(block, axis=1, keepdims=True)
    slot = jnp.concatenate(slots, axis=1).astype(jnp.int32)
    target_ref[...] = owner * capacity + slot
    value = row_ref[...] + 1
    high = (value >> 6).astype(F32)
    low = (value & 63).astype(F32)
    here = lax.broadcasted_iota(jnp.int32, (capacity, length), 0) == slot
    members = member.astype(BF16)
    high_of = nt_dot(members, jnp.where(here, high, 0.0).astype(BF16))
    low_of = nt_dot(members, jnp.where(here, low, 0.0).astype(BF16))
    request_ref[...] = (high_of * 64.0 + low_of).astype(jnp.int32) - 1


def slot_index(owner, offset, owners, capacity):
    length = owner.shape[1]
    return pl.pallas_call(
        index_kernel,
        out_shape=(
            jax.ShapeDtypeStruct((1, length), jnp.int32),
            jax.ShapeDtypeStruct((owners, capacity), jnp.int32),
        ),
        compiler_params=pltpu.CompilerParams(vmem_limit_bytes=8 << 20),
        name="slot_index",
    )(owner, offset)


def lookup_kernel(request_ref, table_ref, out_ref, low_ref, high_ref, total_ref):
    owners, capacity = request_ref.shape
    slots = owners * capacity
    lanes = 128
    step, steps = pl.program_id(0), pl.num_programs(0)
    some = table_ref.shape[0]

    @pl.when(step == 0)
    def _():
        asked = jnp.maximum(request_ref[...] + 1, 0)
        split = jnp.concatenate([(asked >> 6).astype(F32), (asked & 63).astype(F32)], axis=1)
        weight = jnp.where(
            lax.broadcasted_iota(jnp.int32, (2 * capacity, lanes), 0) < capacity, 64.0, 1.0
        ).astype(BF16)
        block = 256

        def expand(index, carry):
            first = index * block
            slot_of = first + lax.broadcasted_iota(jnp.int32, (block, owners), 0)
            owner_at = lax.broadcasted_iota(jnp.int32, (block, owners), 1)
            pick = (slot_of // capacity == owner_at).astype(F32)
            spread = nn_dot(pick.astype(BF16), split.astype(BF16))
            place_at = lax.rem(
                first + lax.broadcasted_iota(jnp.int32, (block, 2 * capacity), 0), capacity
            )
            lane_at = lax.rem(lax.broadcasted_iota(jnp.int32, (block, 2 * capacity), 1), capacity)
            spread = jnp.where(place_at == lane_at, spread, 0.0).astype(BF16)
            wanted = nn_dot(spread, weight).astype(jnp.int32) - 1
            lane_row = lax.broadcasted_iota(jnp.int32, (block, lanes), 1)
            rows = rows_at(index, block)
            high_ref[rows] = (wanted >> 7).astype(F32).astype(BF16)
            low_ref[rows] = ((wanted & (lanes - 1)) == lane_row).astype(F32).astype(BF16)
            return carry

        lax.fori_loop(0, slots // block, expand, 0)

    low, high = low_ref[...], high_ref[...]
    none = jnp.zeros_like(low)
    first = step * (some // lanes)
    hot = [
        jnp.where(high == (first + at).astype(F32).astype(BF16), low, none)
        for at in range(some // lanes)
    ]
    part = nn_dot(jnp.concatenate(hot, axis=1), table_ref[...].astype(BF16))

    @pl.when(step == 0)
    def _():
        total_ref[...] = part

    @pl.when((step > 0) & (step < steps - 1))
    def _():
        total_ref[...] += part

    @pl.when(step == steps - 1)
    def _():
        out_ref[...] = (total_ref[...] + part).astype(BF16)


def look_up(requested, table):
    owners, capacity = requested.shape
    rows, width = table.shape
    slots = owners * capacity
    some = rows // 4
    return pl.pallas_call(
        lookup_kernel,
        grid=(rows // some,),
        in_specs=[
            pl.BlockSpec((owners, capacity), lambda i: (0, 0)),
            pl.BlockSpec((some, width), lambda i: (i, 0)),
        ],
        out_specs=pl.BlockSpec((slots, width), lambda i: (0, 0)),
        out_shape=jax.ShapeDtypeStruct((slots, width), BF16),
        scratch_shapes=[
            pltpu.VMEM((slots, 128), BF16),
            pltpu.VMEM((slots, 128), BF16),
            pltpu.VMEM((slots, width), F32),
        ],
        compiler_params=pltpu.CompilerParams(vmem_limit_bytes=62 << 20),
        name="look_up",
    )(requested, table)


def update_kernel(request_ref, stale_ref, incoming_ref, table_ref, out_ref, low_ref, high_ref):
    block = out_ref.shape[0]
    group, slots = low_ref.shape

    @pl.when(pl.program_id(0) == 0)
    def _():
        asked = request_ref[...]
        row = lax.broadcasted_iota(jnp.int32, (group, slots), 0)
        low_ref[...] = ((asked & (group - 1)) == row).astype(F32).astype(BF16)
        high_ref[...] = jnp.broadcast_to((asked >> (group.bit_length() - 1)).astype(F32), high_ref.shape).astype(BF16)

    low = low_ref[...]
    high = jnp.concatenate([high_ref[...]] * (group // high_ref.shape[0]), axis=0)
    none = jnp.zeros_like(low)
    first = pl.program_id(0) * (block // group)
    hot = [
        jnp.where(high == (first + at).astype(F32).astype(BF16), low, none)
        for at in range(block // group)
    ]
    table_grad = nn_dot(jnp.concatenate(hot, axis=0), incoming_ref[...])
    stale = [as_column(stale_ref[0, at : at + 1, :]) for at in range(stale_ref.shape[1])]
    rate = 0.5 / (1.0 + jnp.concatenate(stale, axis=0))
    out_ref[...] = table_ref[...] - rate * table_grad


def update_table(requested, staleness, incoming, table):
    rows, width = table.shape
    slots = incoming.shape[0]
    block, group = 1024, 256
    return pl.pallas_call(
        update_kernel,
        grid=(rows // block,),
        in_specs=[
            pl.BlockSpec((1, slots), lambda i: (0, 0)),
            pl.BlockSpec((1, block // 128, 128), lambda i: (i, 0, 0)),
            pl.BlockSpec((slots, width), lambda i: (0, 0)),
            pl.BlockSpec((block, width), lambda i: (i, 0)),
        ],
        out_specs=pl.BlockSpec((block, width), lambda i: (i, 0)),
        out_shape=jax.ShapeDtypeStruct((rows, width), F32),
        scratch_shapes=[pltpu.VMEM((group, slots), BF16), pltpu.VMEM((16, slots), BF16)],
        compiler_params=pltpu.CompilerParams(vmem_limit_bytes=32 << 20),
        name="update_table",
    )(requested, staleness.reshape(rows // block, block // 128, 128), incoming, table)


def swap(payload, axes):
    return lax.all_to_all(payload, axes, split_axis=0, concat_axis=0, tiled=True)


def axis_bits(name):
    size = lax.axis_size(name)
    return [1 << bit for bit in range(size.bit_length() - 1)]


def trade(payload, name, flip):
    size = lax.axis_size(name)
    return lax.ppermute(payload, name, [(at, at ^ flip) for at in range(size)])


def spread_plane(piece):
    whole = piece[None]
    for bit in reversed(axis_bits("emb")):
        other = trade(whole, "emb", bit)
        upper = (lax.axis_index("emb") & bit) != 0
        first = jnp.where(upper, other, whole)
        second = jnp.where(upper, whole, other)
        whole = jnp.stack([first, second], axis=1).reshape((-1,) + piece.shape)
    return whole


def reorder_bits(whole):
    bits = len(axis_bits("emb"))
    cube = whole.reshape((2,) * bits + whole.shape[1:])
    order = tuple(reversed(range(bits))) + tuple(range(bits, cube.ndim))
    return cube.transpose(order).reshape(whole.shape)


def gather_weights(w_proj, w_out):
    fsdp_count = lax.axis_size("fsdp")
    emb_count = lax.axis_size("emb")
    layers, rows, _ = w_proj.shape
    piece = layers * rows // emb_count
    first = lax.axis_index("emb") * piece
    mine = jnp.concatenate(
        [
            lax.dynamic_slice_in_dim(shard.reshape(layers * rows, -1), first, piece, 0)
            for shard in (w_proj, w_out)
        ],
        axis=1,
    )
    taken = [mine] + [trade(mine, "fsdp", flip) for flip in range(1, fsdp_count)]
    index = lax.axis_index("fsdp")
    across = []
    for want in range(fsdp_count):
        chosen = taken[0]
        for flip in range(1, fsdp_count):
            chosen = jnp.where((index ^ flip) == want, taken[flip], chosen)
        across.append(chosen)
    every = spread_plane(jnp.stack(across))
    per = emb_count // layers
    whole = every.reshape(layers, per, fsdp_count, piece, -1).transpose(0, 2, 1, 3, 4)
    return whole.reshape(layers, fsdp_count * rows, -1)


def weight_pieces(gw_proj, gw_out):
    if len(gw_proj.shape) == 4:
        return gw_proj
    fsdp_count = lax.axis_size("fsdp")
    emb_count = lax.axis_size("emb")
    rows = gw_proj.shape[0] // fsdp_count
    cols = gw_proj.shape[1] // emb_count
    proj = gw_proj.reshape(fsdp_count, rows, emb_count, cols).transpose(2, 0, 1, 3)
    out = gw_out.reshape(fsdp_count, emb_count, rows // emb_count, -1, cols)
    out = out.transpose(1, 0, 3, 2, 4).reshape(emb_count, fsdp_count, -1, cols)
    return jnp.concatenate([proj, out], axis=2)


def plane_sum_whole(pieces):
    return swap(pieces, "emb").astype(F32).sum(axis=0)


def plane_sum_halving(pieces, ordered):
    bits = axis_bits("emb")
    held = pieces if ordered else reorder_bits(pieces)
    for bit in bits:
        half = held.shape[0] // 2
        upper = (lax.axis_index("emb") & bit) != 0
        low, high = held[:half], held[half:]
        got = trade(jnp.where(upper, low, high).astype(BF16), "emb", bit)
        held = jnp.where(upper, high, low).astype(F32) + got.astype(F32)
    return held[0]


def finish_weights(planes, scale):
    fsdp_count = lax.axis_size("fsdp")
    index = lax.axis_index("fsdp")
    held = planes.astype(BF16)
    total = lax.dynamic_index_in_dim(planes, index, 0, keepdims=False)
    for flip in range(1, fsdp_count):
        leaving = lax.dynamic_index_in_dim(held, index ^ flip, 0, keepdims=False)
        total = total + trade(leaving, "fsdp", flip).astype(F32)
    return spread_plane((total * scale).astype(BF16))


def unpack_weights(every, rows, width):
    emb_count = every.shape[0]
    proj = every[:, :rows].transpose(1, 0, 2).reshape(rows, -1)
    out = every[:, rows:].reshape(emb_count, -1, rows // emb_count, every.shape[2])
    out = out.transpose(0, 2, 1, 3).reshape(rows, width)
    return proj.astype(F32), out.astype(F32)


BLOCK = 256


def normalize(value):
    center = value - jnp.mean(value, axis=-1, keepdims=True)
    inverse = lax.rsqrt(jnp.mean(center * center, axis=-1, keepdims=True) + EPSILON)
    return center * inverse, inverse


def norm_back(gradient, normed, inverse):
    return inverse * (
        gradient
        - jnp.mean(gradient, axis=-1, keepdims=True)
        - normed * jnp.mean(gradient * normed, axis=-1, keepdims=True)
    )


def silu_slope(value):
    half = 0.5 * value
    turn = jnp.tanh(half)
    grown = 1.0 + turn
    return 0.5 * (grown + half * grown * (1.0 - turn))


def rows_at(index, size=BLOCK):
    return pl.ds(pl.multiple_of(index * size, size), size)


def head_masks(width):
    lane = lax.broadcasted_iota(jnp.int32, (1, width), 1) // DH
    return [(lane == head).astype(F32).astype(BF16) for head in range(width // DH)]


def fill_stack(ref, index, value, masks):
    for head, mask in enumerate(masks):
        ref[index, head * BLOCK : (head + 1) * BLOCK, :] = value * mask


def project(hidden_ref, weight, bufs, masks, keep):
    width = hidden_ref.shape[1]
    unit = 0.5 * DH ** (-0.5)

    def step(index, carry):
        rows = rows_at(index)
        normed, _ = normalize(hidden_ref[rows].astype(F32))
        normed = normed.astype(BF16)
        pre = nn_dot(normed, weight[:, : 4 * width])
        if keep:
            bufs["pre"][rows] = pre
            bufs["normed"][:, rows] = normed.astype(F32).T.astype(BF16)
        half = 0.5 * pre
        out = (half + half * jnp.tanh(half)).astype(BF16)
        values = out[:, width : 2 * width]
        queries = out[:, 2 * width : 3 * width] * BF16(unit)
        keys = out[:, 3 * width :]
        bufs["gate"][rows] = out[:, :width]
        bufs["keys"][rows] = keys
        bufs["queries"][rows] = queries
        fill_stack(bufs["q_stack"], index, queries, masks)
        fill_stack(bufs["v_stack"], index, values, masks)
        if keep:
            fill_stack(bufs["k_stack"], index, keys, masks)
            bufs["keys_t"][:, rows] = ((keys * BF16(unit)).astype(F32).T).astype(BF16)
        return carry

    lax.fori_loop(0, hidden_ref.shape[0] // BLOCK, step, 0)


def attend(mix_ref, bufs, heads):
    blocks = mix_ref.shape[0] // BLOCK
    ahead = lax.broadcasted_iota(jnp.int32, (BLOCK, BLOCK), 1) - lax.broadcasted_iota(
        jnp.int32, (BLOCK, BLOCK), 0
    )

    def query_step(at, carry):
        rows = rows_at(at)

        def key_step(to, total):
            keys = bufs["keys"][rows_at(to)]
            visible = ahead <= (at - to) * BLOCK
            parts = []
            for head in range(heads):
                lifted = bufs["q_stack"][at, head * BLOCK : (head + 1) * BLOCK, :]
                half = nt_dot(lifted, keys)
                attn = half + half * jnp.tanh(half)
                parts.append(jnp.where(visible, attn, 0.0).astype(BF16))
            return total + nn_dot(jnp.concatenate(parts, axis=1), bufs["v_stack"][to])

        mix_ref[rows] = lax.fori_loop(
            0, at + 1, key_step, jnp.zeros((BLOCK, mix_ref.shape[1]), F32)
        )
        return carry

    lax.fori_loop(0, blocks, query_step, 0)


def finish_forward(hidden_ref, mix_ref, weight, gate_ref, next_ref):
    width = hidden_ref.shape[1]

    def step(index, carry):
        rows = rows_at(index)
        mixed, _ = normalize(mix_ref[rows])
        gated = (mixed * gate_ref[rows].astype(F32)).astype(BF16)
        branch = nn_dot(gated, weight[:, 4 * width :])
        next_ref[rows] = (hidden_ref[rows].astype(F32) + branch).astype(BF16)
        return carry

    lax.fori_loop(0, hidden_ref.shape[0] // BLOCK, step, 0)


def backward(hidden_ref, grad_in, grad_out, weight, mix_ref, gw_proj_ref, gw_out_ref, bufs, masks, flip):
    length, width = hidden_ref.shape
    heads = len(masks)
    blocks = length // BLOCK
    pre_ref, gpre_ref, gm_ref = bufs["pre"], bufs["gpre"], bufs["gm"]

    def enter(index, carry):
        rows = rows_at(index)
        gradient = grad_in[rows].astype(BF16)
        mixed, inverse = normalize(mix_ref[rows])
        gate = bufs["gate"][rows].astype(F32)
        gated = mixed * gate
        bufs["gated"][:, rows] = gated.T.astype(BF16)
        grad_gated = nt_dot(gradient, weight[:, 4 * width :])
        slope = silu_slope(pre_ref[rows, :width])
        gpre_ref[rows, :width] = (grad_gated * mixed * slope).astype(BF16)
        grad_mix = norm_back(grad_gated * gate, mixed, inverse).astype(BF16)
        gm_ref[rows] = grad_mix
        fill_stack(bufs["g_stack"], index, grad_mix, masks)
        bufs["gq"][:, rows] = jnp.zeros((width, BLOCK), F32)
        bufs["round"][rows] = gradient
        return carry

    lax.fori_loop(0, blocks, enter, 0)
    store_out_pieces(gw_out_ref, gw_proj_ref, nn_dot(bufs["gated"][...], bufs["round"][...]), flip)
    ahead = lax.broadcasted_iota(jnp.int32, (BLOCK, BLOCK), 0) - lax.broadcasted_iota(
        jnp.int32, (BLOCK, BLOCK), 1
    )

    def key_step(to, carry):
        keys_at = rows_at(to)

        def query_step(at, totals):
            grad_values, grad_keys = totals
            cols = rows_at(at)
            queries = bufs["queries"][cols]
            grad_mix = gm_ref[cols]
            visible = ahead <= (at - to) * BLOCK
            attns, grads = [], []
            halves = nt_dot(bufs["k_stack"][to], queries)
            grad_attns = nt_dot(bufs["v_stack"][to], grad_mix)
            for head in range(heads):
                span = slice(head * BLOCK, (head + 1) * BLOCK)
                half = halves[span]
                grad_attn = grad_attns[span]
                turn = jnp.tanh(half)
                grown = 1.0 + turn
                attn = half * grown
                slope = grown + attn * (1.0 - turn)
                attns.append(jnp.where(visible, attn, 0.0).astype(BF16))
                grad_score = jnp.where(visible, grad_attn * slope, 0.0).astype(BF16)
                grads.append(grad_score)
                place = slice(head * DH, (head + 1) * DH)
                bufs["gq"][place, cols] += nn_dot(bufs["keys_t"][place, keys_at], grad_score)
            grad_values += nn_dot(jnp.concatenate(attns, axis=1), bufs["g_stack"][at])
            grad_keys += nn_dot(jnp.concatenate(grads, axis=1), bufs["q_stack"][at])
            return grad_values, grad_keys

        zero = jnp.zeros((BLOCK, width), F32)
        grad_values, grad_keys = lax.fori_loop(to, blocks, query_step, (zero, zero))
        slope = silu_slope(pre_ref[keys_at, width : 2 * width])
        gpre_ref[keys_at, width : 2 * width] = (grad_values * slope).astype(BF16)
        slope = silu_slope(pre_ref[keys_at, 3 * width :])
        gpre_ref[keys_at, 3 * width :] = (grad_keys * slope).astype(BF16)
        return carry

    lax.fori_loop(0, blocks, key_step, 0)

    def leave(index, carry):
        rows = rows_at(index)
        slope = silu_slope(pre_ref[rows, 2 * width : 3 * width])
        gpre_ref[rows, 2 * width : 3 * width] = (bufs["gq"][:, rows].T * slope).astype(BF16)
        grad_normed = nt_dot(gpre_ref[rows, :], weight[:, : 4 * width])
        normed, inverse = normalize(hidden_ref[rows].astype(F32))
        gradient = grad_in[rows].astype(F32) + norm_back(grad_normed, normed, inverse)
        grad_out[rows] = gradient.astype(grad_out.dtype)
        return carry

    lax.fori_loop(0, blocks, leave, 0)

    def weigh(index, carry):
        cols = rows_at(index)
        grad = nn_dot(bufs["normed"][...], gpre_ref[:, cols]).astype(BF16)
        if len(gw_proj_ref.shape) == 2:
            gw_proj_ref[:, cols] = grad
            return carry
        peers, shards, _, lanes = gw_proj_ref.shape
        deep = width // shards
        for part in range(BLOCK // lanes):
            for shard in range(shards):
                gw_proj_ref[turn_bits(index * (BLOCK // lanes) + part, peers, flip), shard, :deep, :] = grad[
                    shard * deep : (shard + 1) * deep, part * lanes : (part + 1) * lanes
                ]
        return carry

    lax.fori_loop(0, 4 * width // BLOCK, weigh, 0)


def turn_bits(index, count, flip):
    if not flip:
        return index
    bits = count.bit_length() - 1
    return sum(((index >> bit) & 1) << (bits - 1 - bit) for bit in range(bits))


def store_out_pieces(gw_out_ref, gw_proj_ref, grad, flip):
    if len(gw_proj_ref.shape) == 2:
        gw_out_ref[...] = grad.astype(BF16)
        return
    peers, shards, rows, lanes = gw_proj_ref.shape
    width = grad.shape[0]
    deep = width // shards
    some = deep // peers
    for shard in range(shards):
        for peer in range(peers):
            first = shard * deep + peer * some
            piece = [
                grad[first : first + some, at : at + lanes] for at in range(0, width, lanes)
            ]
            gw_proj_ref[turn_bits(peer, peers, flip), shard, deep:rows, :] = jnp.concatenate(piece, axis=0).astype(BF16)
    gw_out_ref[...] = jnp.zeros(gw_out_ref.shape, BF16)


def weight_shapes(width, shards, peers):
    deep = width // shards
    lanes = 4 * width // peers
    if lanes == 128 and deep // peers == 8 and deep % 16 == 0:
        rows = deep + deep // peers * width // lanes
        return [
            jax.ShapeDtypeStruct((peers, shards, rows, lanes), BF16),
            jax.ShapeDtypeStruct((8, 128), BF16),
        ]
    return [
        jax.ShapeDtypeStruct((width, 4 * width), BF16),
        jax.ShapeDtypeStruct((width, width), BF16),
    ]


def layer_buffers(length, width):
    heads = width // DH
    blocks = length // BLOCK
    stack = pltpu.VMEM((blocks, heads * BLOCK, width), BF16)
    plain = pltpu.VMEM((length, width), BF16)
    turned = pltpu.VMEM((width, length), BF16)
    return dict(
        pre=pltpu.VMEM((length, 4 * width), F32),
        gpre=pltpu.VMEM((length, 4 * width), BF16),
        normed=turned,
        gated=turned,
        keys_t=turned,
        gq=pltpu.VMEM((width, length), F32),
        gate=plain,
        keys=plain,
        queries=plain,
        gm=plain,
        round=plain,
        q_stack=stack,
        k_stack=stack,
        v_stack=stack,
        g_stack=stack,
    )


def top_kernel(names, layers, target_ref, rows_ref, weights_ref, cot_ref, *refs):
    hidden_refs, refs = refs[:layers], refs[layers:]
    mix_refs, refs = refs[: layers - 1], refs[layers - 1 :]
    grad_ref, gw_proj_ref, gw_out_ref, last_mix_ref = refs[:4]
    bufs = dict(zip(names, refs[4:]))
    width = rows_ref.shape[1]
    masks = head_masks(width)
    place(target_ref, rows_ref, hidden_refs[0])
    for layer in range(layers):
        last = layer == layers - 1
        weight = weights_ref.at[layer]
        mix_ref = last_mix_ref if last else mix_refs[layer]
        project(hidden_refs[layer], weight, bufs, masks, last)
        attend(mix_ref, bufs, len(masks))
        if not last:
            finish_forward(
                hidden_refs[layer], mix_ref, weight, bufs["gate"], hidden_refs[layer + 1]
            )
    backward(
        hidden_refs[-1],
        cot_ref,
        grad_ref,
        weights_ref.at[layers - 1],
        last_mix_ref,
        gw_proj_ref,
        gw_out_ref,
        bufs,
        masks,
        False,
    )


def place(target_ref, rows_ref, out_ref):
    slots = rows_ref.shape[0]

    def step(index, carry):
        rows = rows_at(index)
        wanted = jnp.concatenate(
            [
                as_column(target_ref[:, pl.ds(pl.multiple_of(index * BLOCK + at, 128), 128)])
                for at in range(0, BLOCK, 128)
            ],
            axis=0,
        )
        wanted = jnp.broadcast_to(wanted.astype(jnp.int32), (BLOCK, 128))
        high = (wanted >> 7).astype(F32).astype(BF16)
        lane_row = lax.broadcasted_iota(jnp.int32, (BLOCK, 128), 1)
        low = ((wanted & 127) == lane_row).astype(F32).astype(BF16)
        none = jnp.zeros_like(low)
        hot = [jnp.where(high == BF16(at), low, none) for at in range(slots // 128)]
        out_ref[rows] = nn_dot(jnp.concatenate(hot, axis=1), rows_ref[...]).astype(BF16)
        return carry

    lax.fori_loop(0, out_ref.shape[0] // BLOCK, step, 0)


def run_top(target, rows, weights, cotangent, shards, peers):
    layers = weights.shape[0]
    length, width = cotangent.shape
    buffers = layer_buffers(length, width)
    hidden = jax.ShapeDtypeStruct((length, width), BF16)
    wide = jax.ShapeDtypeStruct((length, width), F32)
    return pl.pallas_call(
        functools.partial(top_kernel, tuple(buffers), layers),
        out_shape=[hidden] * layers
        + [wide] * (layers - 1)
        + [wide]
        + weight_shapes(width, shards, peers),
        scratch_shapes=[pltpu.VMEM((length, width), F32)] + list(buffers.values()),
        compiler_params=pltpu.CompilerParams(vmem_limit_bytes=44 << 20),
        name="forward_and_last_backward",
    )(target, rows, weights, cotangent)


def lower_kernel(
    names, layer, target_ref, hidden_ref, mix_ref, weights_ref, grad_ref, out_ref, gw_proj_ref, gw_out_ref, done_ref, *refs
):
    bufs = dict(zip(names, refs))
    masks = head_masks(hidden_ref.shape[1])
    weight = weights_ref.at[layer]
    project(hidden_ref, weight, bufs, masks, True)
    first = layer == 0
    backward(
        hidden_ref,
        grad_ref,
        done_ref if first else out_ref,
        weight,
        mix_ref,
        gw_proj_ref,
        gw_out_ref,
        bufs,
        masks,
        True,
    )
    if not first:
        return
    length = hidden_ref.shape[0]

    target = jnp.broadcast_to(target_ref[...], (BLOCK, length))
    slot_row = lax.broadcasted_iota(jnp.int32, (BLOCK, length), 0)
    low = ((target & (BLOCK - 1)) == slot_row).astype(F32).astype(BF16)
    high = (target >> (BLOCK.bit_length() - 1)).astype(F32).astype(BF16)
    none = jnp.zeros_like(low)
    group = 4 * BLOCK

    def send(index, carry):
        hot = [
            jnp.where(high == (4 * index + at).astype(F32).astype(BF16), low, none)
            for at in range(4)
        ]
        out_ref[rows_at(index, group)] = nn_dot(
            jnp.concatenate(hot, axis=0), done_ref[...]
        ).astype(BF16)
        return carry

    lax.fori_loop(0, out_ref.shape[0] // group, send, 0)


def run_lower(layer, target, hidden, mix, weights, gradient, slots, shards, peers):
    length, width = hidden.shape
    buffers = layer_buffers(length, width)
    result = (
        jax.ShapeDtypeStruct((slots, width), BF16)
        if layer == 0
        else jax.ShapeDtypeStruct((length, width), F32)
    )
    return pl.pallas_call(
        functools.partial(lower_kernel, tuple(buffers), layer),
        out_shape=[result] + weight_shapes(width, shards, peers),
        scratch_shapes=[pltpu.VMEM((length, width), BF16)] + list(buffers.values()),
        compiler_params=pltpu.CompilerParams(vmem_limit_bytes=44 << 20),
        name="lower_backward",
    )(target, hidden, mix, weights, gradient)


def local(item_table, item_owner, item_row, staleness, w_proj, w_out, out_grad):
    fsdp_count = lax.axis_size("fsdp")
    emb_count = lax.axis_size("emb")
    owners = fsdp_count * emb_count
    length = item_row.shape[1]
    capacity = 2 * length // owners
    width = item_table.shape[1]
    layer_count, shard_rows, _ = w_proj.shape
    slots = owners * capacity
    both = ("fsdp", "emb")
    weights = gather_weights(w_proj, w_out)
    target, request = slot_index(item_owner.reshape(1, length), item_row, owners, capacity)
    requested = swap(request, both)
    looked_up = look_up(requested, item_table)
    returned = swap(looked_up.reshape(owners, capacity, width), both)
    returned, asked = lax.optimization_barrier(
        (returned.reshape(slots, width), requested.reshape(1, slots))
    )
    norm_scale = (owners * length) ** (-0.5)
    outs = run_top(target, returned, weights, out_grad[0], fsdp_count, emb_count)
    hiddens, mixes = outs[:layer_count], outs[layer_count : 2 * layer_count - 1]
    gradient, gw_proj, gw_out = outs[2 * layer_count - 1 :]
    planes = [plane_sum_whole(weight_pieces(gw_proj, gw_out))]
    for layer in reversed(range(layer_count - 1)):
        gradient, gw_proj, gw_out = run_lower(
            layer,
            target,
            hiddens[layer],
            mixes[layer],
            weights,
            gradient,
            slots,
            fsdp_count,
            emb_count,
        )
        pieces = weight_pieces(gw_proj, gw_out)
        planes.insert(0, plane_sum_halving(pieces, len(gw_proj.shape) == 4))
    incoming = swap(gradient.reshape(owners, capacity, width), both)
    incoming = incoming.reshape(slots, width)
    new_table = update_table(asked, staleness, incoming, item_table)
    every = finish_weights(jnp.stack(planes, axis=1), norm_scale)
    sums = [unpack_weights(every[:, at], shard_rows, width) for at in range(layer_count)]
    return (
        new_table,
        jnp.stack([proj for proj, _ in sums]),
        jnp.stack([out for _, out in sums]),
    )


def solution(mesh):
    return jax.shard_map(
        local,
        mesh=mesh,
        in_specs=(
            P(("fsdp", "emb"), None),
            P(("fsdp", "emb"), None, None),
            P(("fsdp", "emb"), None),
            P(("fsdp", "emb")),
            P(None, "fsdp", None),
            P(None, "fsdp", None),
            P(("fsdp", "emb"), None, None),
        ),
        out_specs=(P(("fsdp", "emb"), None), P(None, "fsdp", None), P(None, "fsdp", None)),
        check_vma=False,
    )
```

profile of v0, /device:TPU:0, one launch (start us, length us, event | category | flops | bytes accessed | tf_op | source)
XLA Modules:
  0.0 198.9 jit_solution(11391394525128978388)
XLA Ops:
  1.6 3.1 %collective-permute-start.2 = (bf16[16,1280]{1,0:T(8,128)(2,1)S(1)}, bf16[16,1280]{1,0:T(8,128)(2,1)S(1)}, u32[]{:S(2)}, u32[]{:S(2)}) collective-permute-start(bf16[16,1280]{1,0:T(8,128)(2,1)S(1)} %pad_maximum_fusion.5), channel_id=1, source_target_pairs={{0,8},{8,0},{16,24},{24,16},{1,9},{9,1},{17,25},{25,17},{2,10},{10... | collective-permute-start | bytes 122888 | tf_op jit(solution)/shard_map/ppermute | solution.py:215
  4.7 2.6 %collective-permute-start.1 = (bf16[16,1280]{1,0:T(8,128)(2,1)S(1)}, bf16[16,1280]{1,0:T(8,128)(2,1)S(1)}, u32[]{:S(2)}, u32[]{:S(2)}) collective-permute-start(bf16[16,1280]{1,0:T(8,128)(2,1)S(1)} %pad_maximum_fusion.5), channel_id=1, source_target_pairs={{0,16},{8,24},{16,0},{24,8},{1,17},{9,25},{17,1},{25,9},{2,18},{10... | collective-permute-start | bytes 122888 | tf_op jit(solution)/shard_map/ppermute | solution.py:215
  7.3 3.1 %collective-permute-done.1 = bf16[16,1280]{1,0:T(8,128)(2,1)S(1)} collective-permute-done((bf16[16,1280]{1,0:T(8,128)(2,1)S(1)}, bf16[16,1280]{1,0:T(8,128)(2,1)S(1)}, u32[]{:S(2)}, u32[]{:S(2)}) %collective-permute-start.1) | collective-permute-done | bytes 40992 | tf_op jit(solution)/shard_map/ppermute | solution.py:215
  10.4 2.7 %collective-permute-done = bf16[16,1280]{1,0:T(8,128)(2,1)S(1)} collective-permute-done((bf16[16,1280]{1,0:T(8,128)(2,1)S(1)}, bf16[16,1280]{1,0:T(8,128)(2,1)S(1)}, u32[]{:S(2)}, u32[]{:S(2)}) %collective-permute-start) | collective-permute-done | bytes 40992 | tf_op jit(solution)/shard_map/ppermute | solution.py:215
  13.2 1.6 collective-permute-start.3
  14.8 3.8 %collective-permute-done.3 = bf16[1,4,16,1280]{3,2,1,0:T(8,128)(2,1)S(1)} collective-permute-done((bf16[1,4,16,1280]{3,2,1,0:T(8,128)(2,1)S(1)}, bf16[1,4,16,1280]{3,2,1,0:T(8,128)(2,1)S(1)}, u32[]{:S(2)}, u32[]{:S(2)}) %collective-permute-start.3) | collective-permute-done | bytes 163872 | tf_op jit(solution)/shard_map/ppermute | solution.py:215
  19.4 1.5 collective-permute-start.4
  20.9 1.0 slot_index.1
  21.9 2.5 %all-to-all-start = ((s32[32,1,64]{2,1,0:T(1,128)}), s32[32,1,64]{2,1,0:T(1,128)S(1)}, u32[]{:S(2)}, u32[]{:S(2)}) async-start(s32[32,1,64]{2,1,0:T(1,128)} %bitcast.2), calls=%async_computation | async-start | bytes 32768 | tf_op jit(solution)/shard_map/all_to_all | solution.py:205
  24.5 7.1 %all-to-all-done = s32[32,1,64]{2,1,0:T(1,128)S(1)} async-done(((s32[32,1,64]{2,1,0:T(1,128)}), s32[32,1,64]{2,1,0:T(1,128)S(1)}, u32[]{:S(2)}, u32[]{:S(2)}) %all-to-all-start) | async-done | bytes 8224 | tf_op jit(solution)/shard_map/all_to_all | solution.py:205
  32.2 10.8 %look_up.1 = bf16[2048,256]{1,0:T(8,128)(2,1)} custom-call(s32[32,64]{1,0:T(8,128)} %bitcast.138, f32[4096,256]{1,0:T(8,128)} %table_ref.3), custom_call_target="tpu_custom_call" | custom-call | tf_op jit(solution)/shard_map/look_up/pallas_call | solution.py:139
  43.0 2.8 %all-to-all-start.1 = ((bf16[32,64,256]{2,1,0:T(8,128)(2,1)}), bf16[32,64,256]{2,1,0:T(8,128)(2,1)S(1)}, u32[]{:S(2)}, u32[]{:S(2)}) async-start(bf16[32,64,256]{2,1,0:T(8,128)(2,1)} %bitcast.132), calls=%async_computation.1 | async-start | bytes 2097152 | tf_op jit(solution)/shard_map/all_to_all | solution.py:205
  45.8 1.0 select_bitcast_fusion.3
  49.6 22.2 %all-to-all-done.1 = bf16[32,64,256]{2,1,0:T(8,128)(2,1)S(1)} async-done(((bf16[32,64,256]{2,1,0:T(8,128)(2,1)}), bf16[32,64,256]{2,1,0:T(8,128)(2,1)S(1)}, u32[]{:S(2)}, u32[]{:S(2)}) %all-to-all-start.1) | async-done | bytes 1048608 | tf_op jit(solution)/shard_map/all_to_all | solution.py:205
  71.8 38.6 %forward_and_last_backward.1 = (bf16[1024,256]{1,0:T(8,128)(2,1)S(1)}, bf16[1024,256]{1,0:T(8,128)(2,1)}, f32[1024,256]{1,0:T(8,128)S(1)}, f32[1024,256]{1,0:T(8...) custom-call(s32[1,1024]{1,0:T(1,128)S(1)} %get-tuple-element.15.target_ref, ...), custom_call_target="tpu_custom_call" | custom-call | tf_op jit(solution)/shard_map/forward_and_last_backward/pallas_call | solution.py:646
  110.4 22.1 %lower_backward.1 = (bf16[2048,256]{1,0:T(8,128)(2,1)}, bf16[8,4,80,128]{3,2,1,0:T(8,128)(2,1)S(1)}, bf16[8,128]{1,0:T(8,128)(2,1)}) custom-call(s32[1,1024]{1,0:T(1,128)S(1)} %get-tuple-element.15.target_ref, bf16[1024,256]{1,0:T(8,128)(2,1)S(1)} %get-tuple-element.17.hidden_ref, f32[1024,256]{1,0:T(8,128)S(1)} %get-tuple-element.18.mix_ref, ...), custom_call_target="tpu_custom_call" | custom-call | tf_op jit(solution)/shard_map/lower_backward/pallas_call | solution.py:710
  132.6 1.6 collective-permute-done.6
  134.4 1.5 collective-permute-start.7
  135.9 3.5 %all-to-all-start.3 = ((bf16[8,4,80,128]{3,2,1,0:T(8,128)(2,1)}), bf16[8,4,80,128]{3,2,1,0:T(8,128)(2,1)S(1)}, u32[]{:S(2)}, u32[]{:S(2)}) async-start(bf16[8,4,80,128]{3,2,1,0:T(8,128)(2,1)} %get-tuple-element.22), calls=%async_computation.3 | async-start | bytes 1310720 | tf_op jit(solution)/shard_map/all_to_all | solution.py:205
  139.5 1.2 collective-permute-done.7
  140.7 1.6 collective-permute-start.8
  142.3 8.3 %all-to-all-done.3 = bf16[8,4,80,128]{3,2,1,0:T(8,128)(2,1)S(1)} async-done(((bf16[8,4,80,128]{3,2,1,0:T(8,128)(2,1)}), bf16[8,4,80,128]{3,2,1,0:T(8,128)(2,1)S(1)}, u32[]{:S(2)}, u32[]{:S(2)}) %all-to-all-start.3) | async-done | bytes 655392 | tf_op jit(solution)/shard_map/all_to_all | solution.py:205
  152.1 1.4 collective-permute-start.11
  153.6 1.4 collective-permute-start.10
  155.5 2.5 %collective-permute-done.11 = bf16[2,80,128]{2,1,0:T(8,128)(2,1)S(1)} collective-permute-done((bf16[2,80,128]{2,1,0:T(8,128)(2,1)S(1)}, bf16[2,80,128]{2,1,0:T(8,128)(2,1)S(1)}, u32[]{:S(2)}, u32[]{:S(2)}) %collective-permute-start.11) | collective-permute-done | bytes 40992 | tf_op jit(solution)/shard_map/ppermute | solution.py:215
  159.6 4.4 %all-to-all-start.2 = ((bf16[32,64,256]{2,1,0:T(8,128)(2,1)}), bf16[32,64,256]{2,1,0:T(8,128)(2,1)S(1)}, u32[]{:S(2)}, u32[]{:S(2)}) async-start(bf16[32,64,256]{2,1,0:T(8,128)(2,1)} %bitcast.27), calls=%async_computation.2 | async-start | bytes 2097152 | tf_op jit(solution)/shard_map/all_to_all | solution.py:205
  164.1 1.8 collective-permute-start.13
  165.9 9.7 %collective-permute-done.13 = bf16[2,2,80,128]{3,2,1,0:T(8,128)(2,1)S(1)} collective-permute-done((bf16[2,2,80,128]{3,2,1,0:T(8,128)(2,1)S(1)}, bf16[2,2,80,128]{3,2,1,0:T(8,128)(2,1)S(1)}, u32[]{:S(2)}, u32[]{:S(2)}) %collective-permute-start.13) | collective-permute-done | bytes 81952 | tf_op jit(solution)/shard_map/ppermute | solution.py:215
  175.7 1.4 collective-permute-done.14
  179.2 11.1 %all-to-all-done.2 = bf16[32,64,256]{2,1,0:T(8,128)(2,1)S(1)} async-done(((bf16[32,64,256]{2,1,0:T(8,128)(2,1)}), bf16[32,64,256]{2,1,0:T(8,128)(2,1)S(1)}, u32[]{:S(2)}, u32[]{:S(2)}) %all-to-all-start.2) | async-done | bytes 1048608 | tf_op jit(solution)/shard_map/all_to_all | solution.py:205
  190.3 2.2 %copy-done.1 = f32[4096,256]{1,0:T(8,128)S(1)} copy-done((f32[4096,256]{1,0:T(8,128)S(1)}, f32[4096,256]{1,0:T(8,128)}, u32[]{:S(2)}) %copy-start.1) | copy-done | bytes 4194328
  192.5 6.5 %update_table.1 = f32[4096,256]{1,0:T(8,128)} custom-call(s32[1,2048]{1,0:T(1,128)S(1)} %reshape.115.request_ref, s32[4,8,128]{2,1,0:T(8,128)S(1)} %bitcast.129, bf16[2048,256]{1,0:T(8,128)(2,1)S(1)} %bitcast.127, f32[4096,256]{1,0:T(8,128)S(1)} %copy-done.1), custom_call_target="tpu_custom_call" | custom-call | tf_op jit(solution)/shard_map/update_table/pallas_call | solution.py:187
  (70 shorter events, 11.2 us)
Async XLA Ops:
  0.6 1.0 copy-start
  0.6 20.3 %copy-start.5 = (s32[1,1024]{1,0:T(1,128)S(1)}, s32[1,1024]{1,0:T(1,128)}, u32[]{:S(2)}) copy-start(s32[1,1024]{1,0:T(1,128)} %row_ref.1) | copy-start | bytes 12292
  0.7 20.2 %copy-start.4 = (s32[1,1024,1]{1,2,0:T(1,128)S(1)}, s32[1,1024,1]{1,2,0:T(1,128)}, u32[]{:S(2)}) copy-start(s32[1,1024,1]{1,2,0:T(1,128)} %param.8) | copy-start | bytes 12292
  1.6 5.7 %collective-permute-start.2 = (bf16[16,1280]{1,0:T(8,128)(2,1)S(1)}, bf16[16,1280]{1,0:T(8,128)(2,1)S(1)}, u32[]{:S(2)}, u32[]{:S(2)}) collective-permute-start(bf16[16,1280]{1,0:T(8,128)(2,1)S(1)} %pad_maximum_fusion.5), channel_id=1, source_target_pairs={{0,8},{8,0},{16,24},{24,16},{1,9},{9,1},{17,25},{25,17},{2,10},{10... | collective-permute-start | bytes 122888 | tf_op jit(solution)/shard_map/ppermute | solution.py:215
  4.7 5.7 %collective-permute-start.1 = (bf16[16,1280]{1,0:T(8,128)(2,1)S(1)}, bf16[16,1280]{1,0:T(8,128)(2,1)S(1)}, u32[]{:S(2)}, u32[]{:S(2)}) collective-permute-start(bf16[16,1280]{1,0:T(8,128)(2,1)S(1)} %pad_maximum_fusion.5), channel_id=1, source_target_pairs={{0,16},{8,24},{16,0},{24,8},{1,17},{9,25},{17,1},{25,9},{2,18},{10... | collective-permute-start | bytes 122888 | tf_op jit(solution)/shard_map/ppermute | solution.py:215
  7.3 5.8 %collective-permute-start = (bf16[16,1280]{1,0:T(8,128)(2,1)S(1)}, bf16[16,1280]{1,0:T(8,128)(2,1)S(1)}, u32[]{:S(2)}, u32[]{:S(2)}) collective-permute-start(bf16[16,1280]{1,0:T(8,128)(2,1)S(1)} %pad_maximum_fusion.5), channel_id=1, source_target_pairs={{0,24},{8,16},{16,8},{24,0},{1,25},{9,17},{17,9},{25,1},{2,26},{10... | collective-permute-start | bytes 122888 | tf_op jit(solution)/shard_map/ppermute | solution.py:215
  13.2 5.4 %collective-permute-start.3 = (bf16[1,4,16,1280]{3,2,1,0:T(8,128)(2,1)S(1)}, bf16[1,4,16,1280]{3,2,1,0:T(8,128)(2,1)S(1)}, u32[]{:S(2)}, u32[]{:S(2)}) collective-permute-start(bf16[1,4,16,1280]{3,2,1,0:T(8,128)(2,1)S(1)} %maximum_bitcast_fusion.1), channel_id=1, source_target_pairs={{0,4},{1,5},{2,6},{3,7},{4,0},{5,1},{6,2},{7,3},{8,12},{9,13},{10,... | collective-permute-start | bytes 491528 | tf_op jit(solution)/shard_map/ppermute | solution.py:215
  19.4 26.4 %collective-permute-start.4 = (bf16[2,4,16,1280]{3,2,1,0:T(8,128)(2,1)}, bf16[2,4,16,1280]{3,2,1,0:T(8,128)(2,1)}, u32[]{:S(2)}, u32[]{:S(2)}) collective-permute-start(bf16[2,4,16,1280]{3,2,1,0:T(8,128)(2,1)} %maximum_bitcast_fusion), channel_id=1, source_target_pairs={{0,2},{1,3},{2,0},{3,1},{4,6},{5,7},{6,4},{7,5},{8,10},{9,11},{10,... | collective-permute-start | bytes 983048 | tf_op jit(solution)/shard_map/ppermute | solution.py:215
  21.9 9.7 %all-to-all-start = ((s32[32,1,64]{2,1,0:T(1,128)}), s32[32,1,64]{2,1,0:T(1,128)S(1)}, u32[]{:S(2)}, u32[]{:S(2)}) async-start(s32[32,1,64]{2,1,0:T(1,128)} %bitcast.2), calls=%async_computation | async-start | bytes 32768 | tf_op jit(solution)/shard_map/all_to_all | solution.py:205
  31.6 0.6 copy-start.6
  43.0 28.8 %all-to-all-start.1 = ((bf16[32,64,256]{2,1,0:T(8,128)(2,1)}), bf16[32,64,256]{2,1,0:T(8,128)(2,1)S(1)}, u32[]{:S(2)}, u32[]{:S(2)}) async-start(bf16[32,64,256]{2,1,0:T(8,128)(2,1)} %bitcast.132), calls=%async_computation.1 | async-start | bytes 2097152 | tf_op jit(solution)/shard_map/all_to_all | solution.py:205
  45.8 1.7 copy-start.7
  46.9 2.2 %collective-permute-start.5 = (bf16[4,4,16,1280]{3,2,1,0:T(8,128)(2,1)S(1)}, bf16[4,4,16,1280]{3,2,1,0:T(8,128)(2,1)S(1)}, u32[]{:S(2)}, u32[]{:S(2)}) collective-permute-start(bf16[4,4,16,1280]{3,2,1,0:T(8,128)(2,1)S(1)} %bitcast.133), channel_id=1, source_target_pairs={{0,1},{1,0},{2,3},{3,2},{4,5},{5,4},{6,7},{7,6},{8,9},{9,8},{10,11... | collective-permute-start | bytes 1966088 | tf_op jit(solution)/shard_map/ppermute | solution.py:215
  49.5 22.4 %copy-start.2 = (bf16[1,1024,256]{2,1,0:T(8,128)(2,1)S(1)}, bf16[1,1024,256]{2,1,0:T(8,128)(2,1)}, u32[]{:S(2)}) copy-start(bf16[1,1024,256]{2,1,0:T(8,128)(2,1)} %param.13) | copy-start | bytes 1572868
  132.5 1.7 collective-permute-start.6
  134.4 6.3 %collective-permute-start.7 = (bf16[2,4,80,128]{3,2,1,0:T(8,128)(2,1)S(1)}, bf16[2,4,80,128]{3,2,1,0:T(8,128)(2,1)S(1)}, u32[]{:S(2)}, u32[]{:S(2)}) collective-permute-start(bf16[2,4,80,128]{3,2,1,0:T(8,128)(2,1)S(1)} %select_convert_fusion), channel_id=1, source_target_pairs={{0,2},{1,3},{2,0},{3,1},{4,6},{5,7},{6,4},{7,5},{8,10},{9,11},{10,... | collective-permute-start | bytes 491528 | tf_op jit(solution)/shard_map/ppermute | solution.py:215
  135.9 14.7 %all-to-all-start.3 = ((bf16[8,4,80,128]{3,2,1,0:T(8,128)(2,1)}), bf16[8,4,80,128]{3,2,1,0:T(8,128)(2,1)S(1)}, u32[]{:S(2)}, u32[]{:S(2)}) async-start(bf16[8,4,80,128]{3,2,1,0:T(8,128)(2,1)} %get-tuple-element.22), calls=%async_computation.3 | async-start | bytes 1310720 | tf_op jit(solution)/shard_map/all_to_all | solution.py:205
  140.7 10.6 %collective-permute-start.8 = (bf16[1,4,80,128]{3,2,1,0:T(8,128)(2,1)S(1)}, bf16[1,4,80,128]{3,2,1,0:T(8,128)(2,1)S(1)}, u32[]{:S(2)}, u32[]{:S(2)}) collective-permute-start(bf16[1,4,80,128]{3,2,1,0:T(8,128)(2,1)S(1)} %select_convert_fusion.1), channel_id=1, source_target_pairs={{0,4},{1,5},{2,6},{3,7},{4,0},{5,1},{6,2},{7,3},{8,12},{9,13},{10,... | collective-permute-start | bytes 245768 | tf_op jit(solution)/shard_map/ppermute | solution.py:215
  151.4 4.1 %collective-permute-start.9 = (bf16[2,80,128]{2,1,0:T(8,128)(2,1)S(1)}, bf16[2,80,128]{2,1,0:T(8,128)(2,1)S(1)}, u32[]{:S(2)}, u32[]{:S(2)}) collective-permute-start(bf16[2,80,128]{2,1,0:T(8,128)(2,1)S(1)} %get-tuple-element.35), channel_id=1, source_target_pairs={{0,8},{8,0},{16,24},{24,16},{1,9},{9,1},{17,25},{25,17},{2,10},{10... | collective-permute-start | bytes 122888 | tf_op jit(solution)/shard_map/ppermute | solution.py:215
  152.1 5.9 %collective-permute-start.11 = (bf16[2,80,128]{2,1,0:T(8,128)(2,1)S(1)}, bf16[2,80,128]{2,1,0:T(8,128)(2,1)S(1)}, u32[]{:S(2)}, u32[]{:S(2)}) collective-permute-start(bf16[2,80,128]{2,1,0:T(8,128)(2,1)S(1)} %get-tuple-element.36), channel_id=1, source_target_pairs={{0,24},{8,16},{16,8},{24,0},{1,25},{9,17},{17,9},{25,1},{2,26},{10... | collective-permute-start | bytes 122888 | tf_op jit(solution)/shard_map/ppermute | solution.py:215
  153.6 5.3 %collective-permute-start.10 = (bf16[2,80,128]{2,1,0:T(8,128)(2,1)S(1)}, bf16[2,80,128]{2,1,0:T(8,128)(2,1)S(1)}, u32[]{:S(2)}, u32[]{:S(2)}) collective-permute-start(bf16[2,80,128]{2,1,0:T(8,128)(2,1)S(1)} %get-tuple-element.37), channel_id=1, source_target_pairs={{0,16},{8,24},{16,0},{24,8},{1,17},{9,25},{17,1},{25,9},{2,18},{10... | collective-permute-start | bytes 122888 | tf_op jit(solution)/shard_map/ppermute | solution.py:215
  158.9 5.2 %collective-permute-start.12 = (bf16[1,2,80,128]{3,2,1,0:T(8,128)(2,1)S(1)}, bf16[1,2,80,128]{3,2,1,0:T(8,128)(2,1)S(1)}, u32[]{:S(2)}, u32[]{:S(2)}) collective-permute-start(bf16[1,2,80,128]{3,2,1,0:T(8,128)(2,1)S(1)} %fusion.8), channel_id=1, source_target_pairs={{0,4},{1,5},{2,6},{3,7},{4,0},{5,1},{6,2},{7,3},{8,12},{9,13},{10,... | collective-permute-start | bytes 122888 | tf_op jit(solution)/shard_map/ppermute | solution.py:215
  159.6 30.6 %all-to-all-start.2 = ((bf16[32,64,256]{2,1,0:T(8,128)(2,1)}), bf16[32,64,256]{2,1,0:T(8,128)(2,1)S(1)}, u32[]{:S(2)}, u32[]{:S(2)}) async-start(bf16[32,64,256]{2,1,0:T(8,128)(2,1)} %bitcast.27), calls=%async_computation.2 | async-start | bytes 2097152 | tf_op jit(solution)/shard_map/all_to_all | solution.py:205
  164.1 11.5 %collective-permute-start.13 = (bf16[2,2,80,128]{3,2,1,0:T(8,128)(2,1)S(1)}, bf16[2,2,80,128]{3,2,1,0:T(8,128)(2,1)S(1)}, u32[]{:S(2)}, u32[]{:S(2)}) collective-permute-start(bf16[2,2,80,128]{3,2,1,0:T(8,128)(2,1)S(1)} %maximum_bitcast_fusion.2), channel_id=1, source_target_pairs={{0,2},{1,3},{2,0},{3,1},{4,6},{5,7},{6,4},{7,5},{8,10},{9,11},{10,... | collective-permute-start | bytes 245768 | tf_op jit(solution)/shard_map/ppermute | solution.py:215
  175.7 1.5 collective-permute-start.14
  177.3 13.0 %copy-start.3 = (s32[4096]{0:T(1024)S(1)}, s32[4096]{0:T(1024)}, u32[]{:S(2)}) copy-start(s32[4096]{0:T(1024)} %param.10) | copy-start | bytes 49156
  190.3 2.2 %copy-start.1 = (f32[4096,256]{1,0:T(8,128)S(1)}, f32[4096,256]{1,0:T(8,128)}, u32[]{:S(2)}) copy-start(f32[4096,256]{1,0:T(8,128)} %table_ref.3) | copy-start | bytes 12582916
where the time goes:
time: 199 us
  Pallas kernels  78.9 us (40%)
  waiting for transfers between devices  77.5 us (39%)
  starting transfers between devices  31.6 us (16%)
  local copies, waits for them, and re-layouts  4.96 us (2%)
  other arithmetic  4.95 us (2%)
    all_to_all x4, waiting for transfers between devices, swap(): lax.all_to_all(payload, axes, split_axis=0, concat_axis=0, tiled=True)  48.7 us
    pallas_call x1, Pallas kernels, run_top(): pl.pallas_call(functools.partial(top_kernel, tuple(buffers), layers), out...  38.6 us
    ppermute x15, waiting for transfers between devices, trade(): return lax.ppermute(payload, name, [(at, at ^ flip) for at in range(size)])  28.8 us
    pallas_call x1, Pallas kernels, run_lower(): pl.pallas_call(functools.partial(lower_kernel, tuple(buffers), layer), ou...  22.1 us
    ppermute x15, starting transfers between devices, trade(): return lax.ppermute(payload, name, [(at, at ^ flip) for at in range(size)])  18.2 us
    all_to_all x4, starting transfers between devices, swap(): lax.all_to_all(payload, axes, split_axis=0, concat_axis=0, tiled=True)  13.3 us
    pallas_call x1, Pallas kernels, look_up(): pl.pallas_call(lookup_kernel, grid=(rows // some,), in_specs=[pl.BlockSpe...  10.8 us
    pallas_call x1, Pallas kernels, update_table(): pl.pallas_call(update_kernel, grid=(rows // block,), in_specs=[pl.BlockSp...  6.45 us
  transfers between devices with their start and end apart: 19, of which 16 were waited for; matrix products, arithmetic and copies ran while one was open for 3% of the time, Pallas kernels for 6%

commit v1 on v0

--- a/solution.py
+++ b/solution.py
@@ -73,15 +73,18 @@
     )(owner, offset)
 
 
-def lookup_kernel(request_ref, table_ref, out_ref, low_ref, high_ref, total_ref):
+def lookup_kernel(request_ref, table_ref, out_ref, asked_ref, low_ref, high_ref):
     owners, capacity = request_ref.shape
     slots = owners * capacity
     lanes = 128
-    step, steps = pl.program_id(0), pl.num_programs(0)
+    step = pl.program_id(0)
     some = table_ref.shape[0]
 
     @pl.when(step == 0)
     def _():
+        asked_ref[...] = jnp.concatenate(
+            [request_ref[at : at + 1, :] for at in range(owners)], axis=1
+        )
         asked = jnp.maximum(request_ref[...] + 1, 0)
         split = jnp.concatenate([(asked >> 6).astype(F32), (asked & 63).astype(F32)], axis=1)
         weight = jnp.where(
@@ -89,7 +92,7 @@
         ).astype(BF16)
         block = 256
 
-        def expand(index, carry):
+        for index in range(slots // block):
             first = index * block
             slot_of = first + lax.broadcasted_iota(jnp.int32, (block, owners), 0)
             owner_at = lax.broadcasted_iota(jnp.int32, (block, owners), 1)
@@ -102,33 +105,24 @@
             spread = jnp.where(place_at == lane_at, spread, 0.0).astype(BF16)
             wanted = nn_dot(spread, weight).astype(jnp.int32) - 1
             lane_row = lax.broadcasted_iota(jnp.int32, (block, lanes), 1)
-            rows = rows_at(index, block)
+            rows = slice(first, first + block)
             high_ref[rows] = (wanted >> 7).astype(F32).astype(BF16)
             low_ref[rows] = ((wanted & (lanes - 1)) == lane_row).astype(F32).astype(BF16)
-            return carry
-
-        lax.fori_loop(0, slots // block, expand, 0)
+
+    first = step * (some // lanes)
+
+    @pl.when(step == 0)
+    def _():
+        out_ref[...] = jnp.zeros(out_ref.shape, BF16)
 
     low, high = low_ref[...], high_ref[...]
     none = jnp.zeros_like(low)
-    first = step * (some // lanes)
     hot = [
         jnp.where(high == (first + at).astype(F32).astype(BF16), low, none)
         for at in range(some // lanes)
     ]
-    part = nn_dot(jnp.concatenate(hot, axis=1), table_ref[...].astype(BF16))
-
-    @pl.when(step == 0)
-    def _():
-        total_ref[...] = part
-
-    @pl.when((step > 0) & (step < steps - 1))
-    def _():
-        total_ref[...] += part
-
-    @pl.when(step == steps - 1)
-    def _():
-        out_ref[...] = (total_ref[...] + part).astype(BF16)
+    chunk = table_ref[...].astype(BF16)
+    out_ref[...] += nn_dot(jnp.concatenate(hot, axis=1), chunk).astype(BF16)
 
 
 def look_up(requested, table):
@@ -143,12 +137,17 @@
             pl.BlockSpec((owners, capacity), lambda i: (0, 0)),
             pl.BlockSpec((some, width), lambda i: (i, 0)),
         ],
-        out_specs=pl.BlockSpec((slots, width), lambda i: (0, 0)),
-        out_shape=jax.ShapeDtypeStruct((slots, width), BF16),
+        out_specs=[
+            pl.BlockSpec((slots, width), lambda i: (0, 0)),
+            pl.BlockSpec((1, slots), lambda i: (0, 0)),
+        ],
+        out_shape=[
+            jax.ShapeDtypeStruct((slots, width), BF16),
+            jax.ShapeDtypeStruct((1, slots), jnp.int32),
+        ],
         scratch_shapes=[
             pltpu.VMEM((slots, 128), BF16),
             pltpu.VMEM((slots, 128), BF16),
-            pltpu.VMEM((slots, width), F32),
         ],
         compiler_params=pltpu.CompilerParams(vmem_limit_bytes=62 << 20),
         name="look_up",
@@ -196,7 +195,7 @@
         out_specs=pl.BlockSpec((block, width), lambda i: (i, 0)),
         out_shape=jax.ShapeDtypeStruct((rows, width), F32),
         scratch_shapes=[pltpu.VMEM((group, slots), BF16), pltpu.VMEM((16, slots), BF16)],
-        compiler_params=pltpu.CompilerParams(vmem_limit_bytes=32 << 20),
+        compiler_params=pltpu.CompilerParams(vmem_limit_bytes=62 << 20),
         name="update_table",
     )(requested, staleness.reshape(rows // block, block // 128, 128), incoming, table)
 
@@ -224,13 +223,6 @@
         second = jnp.where(upper, whole, other)
         whole = jnp.stack([first, second], axis=1).reshape((-1,) + piece.shape)
     return whole
-
-
-def reorder_bits(whole):
-    bits = len(axis_bits("emb"))
-    cube = whole.reshape((2,) * bits + whole.shape[1:])
-    order = tuple(reversed(range(bits))) + tuple(range(bits, cube.ndim))
-    return cube.transpose(order).reshape(whole.shape)
 
 
 def gather_weights(w_proj, w_out):
@@ -260,7 +252,12 @@
     return whole.reshape(layers, fsdp_count * rows, -1)
 
 
-def weight_pieces(gw_proj, gw_out):
+def turn_bits(index, count):
+    bits = count.bit_length() - 1
+    return sum(((index >> bit) & 1) << (bits - 1 - bit) for bit in range(bits))
+
+
+def weight_pieces(gw_proj, gw_out, turned):
     if len(gw_proj.shape) == 4:
         return gw_proj
     fsdp_count = lax.axis_size("fsdp")
@@ -270,33 +267,32 @@
     proj = gw_proj.reshape(fsdp_count, rows, emb_count, cols).transpose(2, 0, 1, 3)
     out = gw_out.reshape(fsdp_count, emb_count, rows // emb_count, -1, cols)
     out = out.transpose(1, 0, 3, 2, 4).reshape(emb_count, fsdp_count, -1, cols)
-    return jnp.concatenate([proj, out], axis=2)
+    pieces = jnp.concatenate([proj, out], axis=2)
+    pieces = jnp.take(pieces, jnp.arange(fsdp_count) ^ lax.axis_index("fsdp"), axis=1)
+    if turned:
+        order = turn_bits(jnp.arange(emb_count), emb_count) ^ lax.axis_index("emb")
+        pieces = jnp.take(pieces, order, axis=0)
+    return pieces
 
 
 def plane_sum_whole(pieces):
     return swap(pieces, "emb").astype(F32).sum(axis=0)
 
 
-def plane_sum_halving(pieces, ordered):
-    bits = axis_bits("emb")
-    held = pieces if ordered else reorder_bits(pieces)
-    for bit in bits:
+def plane_sum_halving(pieces):
+    held = pieces
+    for bit in axis_bits("emb"):
         half = held.shape[0] // 2
-        upper = (lax.axis_index("emb") & bit) != 0
-        low, high = held[:half], held[half:]
-        got = trade(jnp.where(upper, low, high).astype(BF16), "emb", bit)
-        held = jnp.where(upper, high, low).astype(F32) + got.astype(F32)
+        got = trade(held[half:].astype(BF16), "emb", bit)
+        held = held[:half].astype(F32) + got.astype(F32)
     return held[0]
 
 
 def finish_weights(planes, scale):
-    fsdp_count = lax.axis_size("fsdp")
-    index = lax.axis_index("fsdp")
+    total = planes[0]
     held = planes.astype(BF16)
-    total = lax.dynamic_index_in_dim(planes, index, 0, keepdims=False)
-    for flip in range(1, fsdp_count):
-        leaving = lax.dynamic_index_in_dim(held, index ^ flip, 0, keepdims=False)
-        total = total + trade(leaving, "fsdp", flip).astype(F32)
+    for flip in range(1, planes.shape[0]):
+        total = total + trade(held[flip], "fsdp", flip).astype(F32)
     return spread_plane((total * scale).astype(BF16))
 
 
@@ -325,11 +321,15 @@
     )
 
 
-def silu_slope(value):
-    half = 0.5 * value
-    turn = jnp.tanh(half)
-    grown = 1.0 + turn
-    return 0.5 * (grown + half * grown * (1.0 - turn))
+def each_block(blocks, step):
+    group = 2 if blocks % 2 == 0 else 1
+
+    def some(index, carry):
+        for at in range(group):
+            step(index * group + at, carry)
+        return carry
+
+    lax.fori_loop(0, blocks // group, some, 0)
 
 
 def rows_at(index, size=BLOCK):
@@ -353,13 +353,15 @@
     def step(index, carry):
         rows = rows_at(index)
         normed, _ = normalize(hidden_ref[rows].astype(F32))
-        normed = normed.astype(BF16)
-        pre = nn_dot(normed, weight[:, : 4 * width])
+        normed = 0.5 * normed
         if keep:
-            bufs["pre"][rows] = pre
-            bufs["normed"][:, rows] = normed.astype(F32).T.astype(BF16)
-        half = 0.5 * pre
-        out = (half + half * jnp.tanh(half)).astype(BF16)
+            bufs["normed"][:, rows] = normed.T.astype(BF16)
+        half = nn_dot(normed.astype(BF16), weight[:, : 4 * width])
+        grown = 1.0 + jnp.tanh(half)
+        out = (half * grown).astype(BF16)
+        if keep:
+            grown = grown.astype(BF16)
+            bufs["slope"][rows] = grown + out * (2.0 - grown)
         values = out[:, width : 2 * width]
         queries = out[:, 2 * width : 3 * width] * BF16(unit)
         keys = out[:, 3 * width :]
@@ -370,10 +372,10 @@
         fill_stack(bufs["v_stack"], index, values, masks)
         if keep:
             fill_stack(bufs["k_stack"], index, keys, masks)
-            bufs["keys_t"][:, rows] = ((keys * BF16(unit)).astype(F32).T).astype(BF16)
+            bufs["keys_t"][:, rows] = (keys * BF16(unit)).T
         return carry
 
-    lax.fori_loop(0, hidden_ref.shape[0] // BLOCK, step, 0)
+    each_block(hidden_ref.shape[0] // BLOCK, step)
 
 
 def attend(mix_ref, bufs, heads):
@@ -382,26 +384,45 @@
         jnp.int32, (BLOCK, BLOCK), 0
     )
 
-    def query_step(at, carry):
-        rows = rows_at(at)
-
-        def key_step(to, total):
-            keys = bufs["keys"][rows_at(to)]
-            visible = ahead <= (at - to) * BLOCK
-            parts = []
-            for head in range(heads):
-                lifted = bufs["q_stack"][at, head * BLOCK : (head + 1) * BLOCK, :]
-                half = nt_dot(lifted, keys)
-                attn = half + half * jnp.tanh(half)
-                parts.append(jnp.where(visible, attn, 0.0).astype(BF16))
-            return total + nn_dot(jnp.concatenate(parts, axis=1), bufs["v_stack"][to])
-
-        mix_ref[rows] = lax.fori_loop(
-            0, at + 1, key_step, jnp.zeros((BLOCK, mix_ref.shape[1]), F32)
-        )
+    def clear(index, carry):
+        mix_ref[rows_at(index)] = jnp.zeros((BLOCK, mix_ref.shape[1]), F32)
         return carry
 
-    lax.fori_loop(0, blocks, query_step, 0)
+    lax.fori_loop(0, blocks, clear, 0)
+
+    def pair(at, to):
+        keys = bufs["keys"][rows_at(to)]
+        visible = (ahead <= (at - to) * BLOCK).astype(F32).astype(BF16)
+        parts = []
+        halves = nt_dot(bufs["q_stack"][at], keys).astype(BF16)
+        for head in range(heads):
+            half = halves[head * BLOCK : (head + 1) * BLOCK]
+            parts.append(half * visible * (1.0 + jnp.tanh(half)))
+        return nn_dot(jnp.concatenate(parts, axis=1), bufs["v_stack"][to])
+
+    def add(at, to, total):
+        mix_ref[rows_at(at)] += total
+
+    each_pair(blocks, pair, add)
+
+
+def each_pair(blocks, pair, add):
+    count = blocks * (blocks + 1) // 2
+    group = 5 if count % 5 == 0 else 1
+
+    def step(index, place):
+        at, to = place
+        work = []
+        for _ in range(group):
+            work.append((at, to, pair(at, to)))
+            done = to == at
+            to = jnp.where(done, 0, to + 1)
+            at = jnp.where(done, at + 1, at)
+        for item in work:
+            add(*item)
+        return at, to
+
+    lax.fori_loop(0, count // group, step, (jnp.int32(0), jnp.int32(0)))
 
 
 def finish_forward(hidden_ref, mix_ref, weight, gate_ref, next_ref):
@@ -418,11 +439,11 @@
     lax.fori_loop(0, hidden_ref.shape[0] // BLOCK, step, 0)
 
 
-def backward(hidden_ref, grad_in, grad_out, weight, mix_ref, gw_proj_ref, gw_out_ref, bufs, masks, flip):
+def backward(hidden_ref, grad_in, grad_out, weight, mix_ref, gw_proj_ref, gw_out_ref, bufs, masks, here, flip):
     length, width = hidden_ref.shape
     heads = len(masks)
     blocks = length // BLOCK
-    pre_ref, gpre_ref, gm_ref = bufs["pre"], bufs["gpre"], bufs["gm"]
+    slope_ref, gpre_ref, gm_ref = bufs["slope"], bufs["gpre"], bufs["gm"]
 
     def enter(index, carry):
         rows = rows_at(index)
@@ -432,71 +453,65 @@
         gated = mixed * gate
         bufs["gated"][:, rows] = gated.T.astype(BF16)
         grad_gated = nt_dot(gradient, weight[:, 4 * width :])
-        slope = silu_slope(pre_ref[rows, :width])
-        gpre_ref[rows, :width] = (grad_gated * mixed * slope).astype(BF16)
+        gpre_ref[rows, :width] = (grad_gated * mixed).astype(BF16) * slope_ref[rows, :width]
         grad_mix = norm_back(grad_gated * gate, mixed, inverse).astype(BF16)
         gm_ref[rows] = grad_mix
         fill_stack(bufs["g_stack"], index, grad_mix, masks)
         bufs["gq"][:, rows] = jnp.zeros((width, BLOCK), F32)
+        bufs["gv"][rows] = jnp.zeros((BLOCK, width), F32)
+        bufs["gk"][rows] = jnp.zeros((BLOCK, width), F32)
         bufs["round"][rows] = gradient
         return carry
 
-    lax.fori_loop(0, blocks, enter, 0)
-    store_out_pieces(gw_out_ref, gw_proj_ref, nn_dot(bufs["gated"][...], bufs["round"][...]), flip)
+    each_block(blocks, enter)
+    store_out_pieces(gw_out_ref, gw_proj_ref, nn_dot(bufs["gated"][...], bufs["round"][...]), here, flip)
     ahead = lax.broadcasted_iota(jnp.int32, (BLOCK, BLOCK), 0) - lax.broadcasted_iota(
         jnp.int32, (BLOCK, BLOCK), 1
     )
 
-    def key_step(to, carry):
-        keys_at = rows_at(to)
-
-        def query_step(at, totals):
-            grad_values, grad_keys = totals
-            cols = rows_at(at)
-            queries = bufs["queries"][cols]
-            grad_mix = gm_ref[cols]
-            visible = ahead <= (at - to) * BLOCK
-            attns, grads = [], []
-            halves = nt_dot(bufs["k_stack"][to], queries)
-            grad_attns = nt_dot(bufs["v_stack"][to], grad_mix)
-            for head in range(heads):
-                span = slice(head * BLOCK, (head + 1) * BLOCK)
-                half = halves[span]
-                grad_attn = grad_attns[span]
-                turn = jnp.tanh(half)
-                grown = 1.0 + turn
-                attn = half * grown
-                slope = grown + attn * (1.0 - turn)
-                attns.append(jnp.where(visible, attn, 0.0).astype(BF16))
-                grad_score = jnp.where(visible, grad_attn * slope, 0.0).astype(BF16)
-                grads.append(grad_score)
-                place = slice(head * DH, (head + 1) * DH)
-                bufs["gq"][place, cols] += nn_dot(bufs["keys_t"][place, keys_at], grad_score)
-            grad_values += nn_dot(jnp.concatenate(attns, axis=1), bufs["g_stack"][at])
-            grad_keys += nn_dot(jnp.concatenate(grads, axis=1), bufs["q_stack"][at])
-            return grad_values, grad_keys
-
-        zero = jnp.zeros((BLOCK, width), F32)
-        grad_values, grad_keys = lax.fori_loop(to, blocks, query_step, (zero, zero))
-        slope = silu_slope(pre_ref[keys_at, width : 2 * width])
-        gpre_ref[keys_at, width : 2 * width] = (grad_values * slope).astype(BF16)
-        slope = silu_slope(pre_ref[keys_at, 3 * width :])
-        gpre_ref[keys_at, 3 * width :] = (grad_keys * slope).astype(BF16)
-        return carry
-
-    lax.fori_loop(0, blocks, key_step, 0)
+    def pair(at, to):
+        keys_at, cols = rows_at(to), rows_at(at)
+        visible = (ahead <= (at - to) * BLOCK).astype(F32).astype(BF16)
+        attns, grads, turned = [], [], []
+        halves = nt_dot(bufs["k_stack"][to], bufs["queries"][cols]).astype(BF16)
+        grad_attns = nt_dot(bufs["v_stack"][to], gm_ref[cols]).astype(BF16)
+        for head in range(heads):
+            span = slice(head * BLOCK, (head + 1) * BLOCK)
+            half = halves[span]
+            turn = jnp.tanh(half)
+            grown = 1.0 + turn
+            attn = half * grown
+            attns.append(attn * visible)
+            grads.append(grad_attns[span] * visible * (grown + attn * (1.0 - turn)))
+            place = slice(head * DH, (head + 1) * DH)
+            turned.append(nn_dot(bufs["keys_t"][place, keys_at], grads[-1]))
+        return (
+            nn_dot(jnp.concatenate(attns, axis=1), bufs["g_stack"][at]),
+            nn_dot(jnp.concatenate(grads, axis=1), bufs["q_stack"][at]),
+            turned,
+        )
+
+    def add(at, to, totals):
+        keys_at, cols = rows_at(to), rows_at(at)
+        bufs["gv"][keys_at] += totals[0]
+        bufs["gk"][keys_at] += totals[1]
+        for head in range(heads):
+            bufs["gq"][head * DH : (head + 1) * DH, cols] += totals[2][head]
+
+    each_pair(blocks, pair, add)
 
     def leave(index, carry):
         rows = rows_at(index)
-        slope = silu_slope(pre_ref[rows, 2 * width : 3 * width])
-        gpre_ref[rows, 2 * width : 3 * width] = (bufs["gq"][:, rows].T * slope).astype(BF16)
+        for at, grad in enumerate((bufs["gv"][rows], bufs["gq"][:, rows].T, bufs["gk"][rows])):
+            cols = slice((at + 1) * width, (at + 2) * width)
+            gpre_ref[rows, cols] = grad.astype(BF16) * slope_ref[rows, cols]
         grad_normed = nt_dot(gpre_ref[rows, :], weight[:, : 4 * width])
         normed, inverse = normalize(hidden_ref[rows].astype(F32))
-        gradient = grad_in[rows].astype(F32) + norm_back(grad_normed, normed, inverse)
+        gradient = grad_in[rows].astype(F32) + norm_back(grad_normed, normed, 0.5 * inverse)
         grad_out[rows] = gradient.astype(grad_out.dtype)
         return carry
 
-    lax.fori_loop(0, blocks, leave, 0)
+    each_block(blocks, leave)
 
     def weigh(index, carry):
         cols = rows_at(index)
@@ -508,7 +523,8 @@
         deep = width // shards
         for part in range(BLOCK // lanes):
             for shard in range(shards):
-                gw_proj_ref[turn_bits(index * (BLOCK // lanes) + part, peers, flip), shard, :deep, :] = grad[
+                slot = peer_slot(index * (BLOCK // lanes) + part, peers, here, flip)
+                gw_proj_ref[slot, shard ^ here[0], :deep, :] = grad[
                     shard * deep : (shard + 1) * deep, part * lanes : (part + 1) * lanes
                 ]
         return carry
@@ -516,14 +532,11 @@
     lax.fori_loop(0, 4 * width // BLOCK, weigh, 0)
 
 
-def turn_bits(index, count, flip):
-    if not flip:
-        return index
-    bits = count.bit_length() - 1
-    return sum(((index >> bit) & 1) << (bits - 1 - bit) for bit in range(bits))
-
-
-def store_out_pieces(gw_out_ref, gw_proj_ref, grad, flip):
+def peer_slot(peer, peers, here, flip):
+    return turn_bits(peer ^ here[1], peers) if flip else peer
+
+
+def store_out_pieces(gw_out_ref, gw_proj_ref, grad, here, flip):
     if len(gw_proj_ref.shape) == 2:
         gw_out_ref[...] = grad.astype(BF16)
         return
@@ -537,7 +550,7 @@
             piece = [
                 grad[first : first + some, at : at + lanes] for at in range(0, width, lanes)
             ]
-            gw_proj_ref[turn_bits(peer, peers, flip), shard, deep:rows, :] = jnp.concatenate(piece, axis=0).astype(BF16)
+            gw_proj_ref[peer_slot(peer, peers, here, flip), shard ^ here[0], deep:rows, :] = jnp.concatenate(piece, axis=0).astype(BF16)
     gw_out_ref[...] = jnp.zeros(gw_out_ref.shape, BF16)
 
 
@@ -563,12 +576,14 @@
     plain = pltpu.VMEM((length, width), BF16)
     turned = pltpu.VMEM((width, length), BF16)
     return dict(
-        pre=pltpu.VMEM((length, 4 * width), F32),
+        slope=pltpu.VMEM((length, 4 * width), BF16),
         gpre=pltpu.VMEM((length, 4 * width), BF16),
         normed=turned,
         gated=turned,
         keys_t=turned,
         gq=pltpu.VMEM((width, length), F32),
+        gv=pltpu.VMEM((length, width), F32),
+        gk=pltpu.VMEM((length, width), F32),
         gate=plain,
         keys=plain,
         queries=plain,
@@ -581,14 +596,14 @@
     )
 
 
-def top_kernel(names, layers, target_ref, rows_ref, weights_ref, cot_ref, *refs):
+def top_kernel(names, layers, here_ref, target_ref, rows_ref, weights_ref, cot_ref, *refs):
     hidden_refs, refs = refs[:layers], refs[layers:]
     mix_refs, refs = refs[: layers - 1], refs[layers - 1 :]
-    grad_ref, gw_proj_ref, gw_out_ref, last_mix_ref = refs[:4]
-    bufs = dict(zip(names, refs[4:]))
+    grad_ref, gw_proj_ref, gw_out_ref, last_mix_ref, low_ref, high_ref = refs[:6]
+    bufs = dict(zip(names, refs[6:]))
     width = rows_ref.shape[1]
     masks = head_masks(width)
-    place(target_ref, rows_ref, hidden_refs[0])
+    place(target_ref, rows_ref, hidden_refs[0], low_ref, high_ref)
     for layer in range(layers):
         last = layer == layers - 1
         weight = weights_ref.at[layer]
@@ -609,35 +624,43 @@
         gw_out_ref,
         bufs,
         masks,
+        (here_ref[0], here_ref[1]),
         False,
     )
 
 
-def place(target_ref, rows_ref, out_ref):
-    slots = rows_ref.shape[0]
+def place(target_ref, rows_ref, out_ref, low_ref, high_ref):
+    length = out_ref.shape[0]
+    lanes = 128
+    for at in range(0, length, lanes):
+        rows = slice(at, at + lanes)
+        wanted = as_column(target_ref[:, rows]).astype(jnp.int32)
+        wanted = jnp.broadcast_to(wanted, (lanes, lanes))
+        high_ref[rows] = (wanted >> 7).astype(F32).astype(BF16)
+        lane_row = lax.broadcasted_iota(jnp.int32, (lanes, lanes), 1)
+        low_ref[rows] = ((wanted & (lanes - 1)) == lane_row).astype(F32).astype(BF16)
+    out_ref[...] = jnp.zeros(out_ref.shape, BF16)
 
     def step(index, carry):
-        rows = rows_at(index)
-        wanted = jnp.concatenate(
-            [
-                as_column(target_ref[:, pl.ds(pl.multiple_of(index * BLOCK + at, 128), 128)])
-                for at in range(0, BLOCK, 128)
-            ],
-            axis=0,
-        )
-        wanted = jnp.broadcast_to(wanted.astype(jnp.int32), (BLOCK, 128))
-        high = (wanted >> 7).astype(F32).astype(BF16)
-        lane_row = lax.broadcasted_iota(jnp.int32, (BLOCK, 128), 1)
-        low = ((wanted & 127) == lane_row).astype(F32).astype(BF16)
+        low, high = low_ref[...], high_ref[...]
         none = jnp.zeros_like(low)
-        hot = [jnp.where(high == BF16(at), low, none) for at in range(slots // 128)]
-        out_ref[rows] = nn_dot(jnp.concatenate(hot, axis=1), rows_ref[...]).astype(BF16)
+        hot = [
+            jnp.where(high == (2 * index + side).astype(F32).astype(BF16), low, none)
+            for side in range(2)
+        ]
+        chunk = rows_ref[rows_at(index, 2 * lanes)]
+        out_ref[...] += nn_dot(jnp.concatenate(hot, axis=1), chunk).astype(BF16)
         return carry
 
-    lax.fori_loop(0, out_ref.shape[0] // BLOCK, step, 0)
-
-
-def run_top(target, rows, weights, cotangent, shards, peers):
+    lax.fori_loop(0, rows_ref.shape[0] // (2 * lanes), step, 0)
+
+
+def in_memory(count):
+    whole = pl.BlockSpec(memory_space=pltpu.VMEM)
+    return [pl.BlockSpec(memory_space=pltpu.SMEM)] + [whole] * (count - 1)
+
+
+def run_top(here, target, rows, weights, cotangent, shards, peers):
     layers = weights.shape[0]
     length, width = cotangent.shape
     buffers = layer_buffers(length, width)
@@ -645,18 +668,21 @@
     wide = jax.ShapeDtypeStruct((length, width), F32)
     return pl.pallas_call(
         functools.partial(top_kernel, tuple(buffers), layers),
+        in_specs=in_memory(5),
         out_shape=[hidden] * layers
         + [wide] * (layers - 1)
         + [wide]
         + weight_shapes(width, shards, peers),
-        scratch_shapes=[pltpu.VMEM((length, width), F32)] + list(buffers.values()),
-        compiler_params=pltpu.CompilerParams(vmem_limit_bytes=44 << 20),
+        scratch_shapes=[pltpu.VMEM((length, width), F32)]
+        + [pltpu.VMEM((length, 128), BF16)] * 2
+        + list(buffers.values()),
+        compiler_params=pltpu.CompilerParams(vmem_limit_bytes=62 << 20),
         name="forward_and_last_backward",
-    )(target, rows, weights, cotangent)
+    )(here, target, rows, weights, cotangent)
 
 
 def lower_kernel(
-    names, layer, target_ref, hidden_ref, mix_ref, weights_ref, grad_ref, out_ref, gw_proj_ref, gw_out_ref, done_ref, *refs
+    names, layer, here_ref, target_ref, hidden_ref, mix_ref, weights_ref, grad_ref, out_ref, gw_proj_ref, gw_out_ref, done_ref, *refs
 ):
     bufs = dict(zip(names, refs))
     masks = head_masks(hidden_ref.shape[1])
@@ -673,6 +699,7 @@
         gw_out_ref,
         bufs,
         masks,
+        (here_ref[0], here_ref[1]),
         True,
     )
     if not first:
@@ -699,7 +726,7 @@
     lax.fori_loop(0, out_ref.shape[0] // group, send, 0)
 
 
-def run_lower(layer, target, hidden, mix, weights, gradient, slots, shards, peers):
+def run_lower(layer, here, target, hidden, mix, weights, gradient, slots, shards, peers):
     length, width = hidden.shape
     buffers = layer_buffers(length, width)
     result = (
@@ -709,11 +736,12 @@
     )
     return pl.pallas_call(
         functools.partial(lower_kernel, tuple(buffers), layer),
+        in_specs=in_memory(6),
         out_shape=[result] + weight_shapes(width, shards, peers),
         scratch_shapes=[pltpu.VMEM((length, width), BF16)] + list(buffers.values()),
-        compiler_params=pltpu.CompilerParams(vmem_limit_bytes=44 << 20),
+        compiler_params=pltpu.CompilerParams(vmem_limit_bytes=62 << 20),
         name="lower_backward",
-    )(target, hidden, mix, weights, gradient)
+    )(here, target, hidden, mix, weights, gradient)
 
 
 def local(item_table, item_owner, item_row, staleness, w_proj, w_out, out_grad):
@@ -729,19 +757,19 @@
     weights = gather_weights(w_proj, w_out)
     target, request = slot_index(item_owner.reshape(1, length), item_row, owners, capacity)
     requested = swap(request, both)
-    looked_up = look_up(requested, item_table)
+    looked_up, asked = look_up(requested.reshape(owners, capacity), item_table)
     returned = swap(looked_up.reshape(owners, capacity, width), both)
-    returned, asked = lax.optimization_barrier(
-        (returned.reshape(slots, width), requested.reshape(1, slots))
-    )
+    returned = returned.reshape(slots, width)
+    here = jnp.stack([lax.axis_index("fsdp"), lax.axis_index("emb")]).astype(jnp.int32)
     norm_scale = (owners * length) ** (-0.5)
-    outs = run_top(target, returned, weights, out_grad[0], fsdp_count, emb_count)
+    outs = run_top(here, target, returned, weights, out_grad[0], fsdp_count, emb_count)
     hiddens, mixes = outs[:layer_count], outs[layer_count : 2 * layer_count - 1]
     gradient, gw_proj, gw_out = outs[2 * layer_count - 1 :]
-    planes = [plane_sum_whole(weight_pieces(gw_proj, gw_out))]
+    planes = [plane_sum_whole(weight_pieces(gw_proj, gw_out, False))]
     for layer in reversed(range(layer_count - 1)):
         gradient, gw_proj, gw_out = run_lower(
             layer,
+            here,
             target,
             hiddens[layer],
             mixes[layer],
@@ -751,8 +779,8 @@
             fsdp_count,
             emb_count,
         )
-        pieces = weight_pieces(gw_proj, gw_out)
-        planes.insert(0, plane_sum_halving(pieces, len(gw_proj.shape) == 4))
+        pieces = weight_pieces(gw_proj, gw_out, True)
+        planes.insert(0, plane_sum_halving(pieces))
     incoming = swap(gradient.reshape(owners, capacity, width), both)
     incoming = incoming.reshape(slots, width)
     new_table = update_table(asked, staleness, incoming, item_table)

time: 199 us -> 193 us (0.970)
  Pallas kernels: 78.9 us -> 69.2 us
  waiting for transfers between devices: 77.5 us -> 79.9 us
    ppermute x15, waiting for transfers between devices: 28.8 us -> 40.5 us  [trade(): return lax.ppermute(payload, name, [(at, at ^ flip) for at in range(size)])]
    all_to_all x4, waiting for transfers between devices: 48.7 us -> 39.4 us  [swap(): lax.all_to_all(payload, axes, split_axis=0, concat_axis=0, tiled=True)]
    pallas_call x2, Pallas kernels: 60.7 us -> 51.6 us  [the longest x1 31.5 us: run_top(): pl.pallas_call(functools.partial(top_kernel, tuple(buffers), layers), in_...]
    pallas_call x1, Pallas kernels: 10.8 us -> 8.24 us  [look_up(): pl.pallas_call(lookup_kernel, grid=(rows // some,), in_specs=[pl.BlockSpe...]
  transfers between devices with their start and end apart: 19 -> 19, of which waited for: 16 -> 14; matrix products, arithmetic and copies ran while one was open for 3% -> 3% of each run, Pallas kernels for 6% -> 5%
where the time goes in v1:
time: 193 us; the launch traced here: 192 us
  waiting for transfers between devices  79.9 us (41%)
  Pallas kernels  69.2 us (36%)
  starting transfers between devices  31.4 us (16%)
  local copies, waits for them, and re-layouts  6.91 us (4%)
  other arithmetic  4.03 us (2%)
    ppermute x15, waiting for transfers between devices, trade(): return lax.ppermute(payload, name, [(at, at ^ flip) for at in range(size)])  40.5 us
    all_to_all x4, waiting for transfers between devices, swap(): lax.all_to_all(payload, axes, split_axis=0, concat_axis=0, tiled=True)  39.4 us
    pallas_call x1, Pallas kernels, run_top(): pl.pallas_call(functools.partial(top_kernel, tuple(buffers), layers), in_...  31.5 us
    pallas_call x1, Pallas kernels, run_lower(): pl.pallas_call(functools.partial(lower_kernel, tuple(buffers), layer), in...  20 us
    ppermute x15, starting transfers between devices, trade(): return lax.ppermute(payload, name, [(at, at ^ flip) for at in range(size)])  19.6 us
    all_to_all x4, starting transfers between devices, swap(): lax.all_to_all(payload, axes, split_axis=0, concat_axis=0, tiled=True)  11.8 us
    pallas_call x1, Pallas kernels, update_table(): pl.pallas_call(update_kernel, grid=(rows // block,), in_specs=[pl.BlockSp...  8.38 us
    pallas_call x1, Pallas kernels, look_up(): pl.pallas_call(lookup_kernel, grid=(rows // some,), in_specs=[pl.BlockSpe...  8.24 us
  transfers between devices with their start and end apart: 19, of which 14 were waited for; matrix products, arithmetic and copies ran while one was open for 3% of the time, Pallas kernels for 5%

profile of v1, /device:TPU:0, one launch (start us, length us, event | category | flops | bytes accessed | tf_op | source)
XLA Modules:
  0.0 192.4 jit_solution(3083106331901285604)
XLA Ops:
  1.6 3.1 %collective-permute-start.2 = (bf16[16,1280]{1,0:T(8,128)(2,1)S(1)}, bf16[16,1280]{1,0:T(8,128)(2,1)S(1)}, u32[]{:S(2)}, u32[]{:S(2)}) collective-permute-start(bf16[16,1280]{1,0:T(8,128)(2,1)S(1)} %pad_maximum_fusion.5), channel_id=1, source_target_pairs={{0,8},{8,0},{16,24},{24,16},{1,9},{9,1},{17,25},{25,17},{2,10},{10... | collective-permute-start | bytes 122888 | tf_op jit(solution)/shard_map/ppermute | solution.py:214
  4.7 2.6 %collective-permute-start.1 = (bf16[16,1280]{1,0:T(8,128)(2,1)S(1)}, bf16[16,1280]{1,0:T(8,128)(2,1)S(1)}, u32[]{:S(2)}, u32[]{:S(2)}) collective-permute-start(bf16[16,1280]{1,0:T(8,128)(2,1)S(1)} %pad_maximum_fusion.5), channel_id=1, source_target_pairs={{0,16},{8,24},{16,0},{24,8},{1,17},{9,25},{17,1},{25,9},{2,18},{10... | collective-permute-start | bytes 122888 | tf_op jit(solution)/shard_map/ppermute | solution.py:214
  7.3 3.1 %collective-permute-done.1 = bf16[16,1280]{1,0:T(8,128)(2,1)S(1)} collective-permute-done((bf16[16,1280]{1,0:T(8,128)(2,1)S(1)}, bf16[16,1280]{1,0:T(8,128)(2,1)S(1)}, u32[]{:S(2)}, u32[]{:S(2)}) %collective-permute-start.1) | collective-permute-done | bytes 40992 | tf_op jit(solution)/shard_map/ppermute | solution.py:214
  10.4 2.7 %collective-permute-done = bf16[16,1280]{1,0:T(8,128)(2,1)S(1)} collective-permute-done((bf16[16,1280]{1,0:T(8,128)(2,1)S(1)}, bf16[16,1280]{1,0:T(8,128)(2,1)S(1)}, u32[]{:S(2)}, u32[]{:S(2)}) %collective-permute-start) | collective-permute-done | bytes 40992 | tf_op jit(solution)/shard_map/ppermute | solution.py:214
  13.2 1.6 collective-permute-start.3
  14.8 3.8 %collective-permute-done.3 = bf16[1,4,16,1280]{3,2,1,0:T(8,128)(2,1)S(1)} collective-permute-done((bf16[1,4,16,1280]{3,2,1,0:T(8,128)(2,1)S(1)}, bf16[1,4,16,1280]{3,2,1,0:T(8,128)(2,1)S(1)}, u32[]{:S(2)}, u32[]{:S(2)}) %collective-permute-start.3) | collective-permute-done | bytes 163872 | tf_op jit(solution)/shard_map/ppermute | solution.py:214
  18.7 1.6 collective-permute-start.4
  21.8 2.5 %all-to-all-start = ((s32[32,1,64]{2,1,0:T(1,128)}), s32[32,1,64]{2,1,0:T(1,128)S(1)}, u32[]{:S(2)}, u32[]{:S(2)}) async-start(s32[32,1,64]{2,1,0:T(1,128)} %bitcast.2), calls=%async_computation | async-start | bytes 32768 | tf_op jit(solution)/shard_map/all_to_all | solution.py:204
  24.4 7.1 %all-to-all-done = s32[32,1,64]{2,1,0:T(1,128)S(1)} async-done(((s32[32,1,64]{2,1,0:T(1,128)}), s32[32,1,64]{2,1,0:T(1,128)S(1)}, u32[]{:S(2)}, u32[]{:S(2)}) %all-to-all-start) | async-done | bytes 8224 | tf_op jit(solution)/shard_map/all_to_all | solution.py:204
  32.1 8.2 %look_up.1 = (bf16[2048,256]{1,0:T(8,128)(2,1)}, s32[1,2048]{1,0:T(1,128)}) custom-call(s32[32,64]{1,0:T(8,128)} %bitcast.144, f32[4096,256]{1,0:T(8,128)} %table_ref.3), custom_call_target="tpu_custom_call" | custom-call | tf_op jit(solution)/shard_map/look_up/pallas_call | solution.py:133
  40.3 2.8 %all-to-all-start.1 = ((bf16[32,64,256]{2,1,0:T(8,128)(2,1)}), bf16[32,64,256]{2,1,0:T(8,128)(2,1)S(1)}, u32[]{:S(2)}, u32[]{:S(2)}) async-start(bf16[32,64,256]{2,1,0:T(8,128)(2,1)} %bitcast.141), calls=%async_computation.1 | async-start | bytes 2097152 | tf_op jit(solution)/shard_map/all_to_all | solution.py:204
  43.2 1.0 select_bitcast_fusion.3
  45.0 1.4 collective-permute-done.5
  46.8 1.2 copy.46
  48.0 21.2 %all-to-all-done.1 = bf16[32,64,256]{2,1,0:T(8,128)(2,1)S(1)} async-done(((bf16[32,64,256]{2,1,0:T(8,128)(2,1)}), bf16[32,64,256]{2,1,0:T(8,128)(2,1)S(1)}, u32[]{:S(2)}, u32[]{:S(2)}) %all-to-all-start.1) | async-done | bytes 1048608 | tf_op jit(solution)/shard_map/all_to_all | solution.py:204
  70.2 31.5 %forward_and_last_backward.1 = (bf16[1024,256]{1,0:T(8,128)(2,1)}, bf16[1024,256]{1,0:T(8,128)(2,1)}, f32[1024,256]{1,0:T(8,128)}, f32[1024,256]{1,0:T(8,128)}, ...) custom-call(s32[2]{0:T(128)} %pad_add_fusion.here_ref, s32[1,1024]{1,0:T(1,128)} %copy-done.1, ...), custom_call_target="tpu_custom_call" | custom-call | tf_op jit(solution)/shard_map/forward_and_last_backward/pallas_call | solution.py:669
  101.7 20.0 %lower_backward.1 = (bf16[2048,256]{1,0:T(8,128)(2,1)}, bf16[8,4,80,128]{3,2,1,0:T(8,128)(2,1)}, bf16[8,128]{1,0:T(8,128)(2,1)}) custom-call(s32[2]{0:T(128)} %pad_add_fusion.here_ref, s32[1,1024]{1,0:T(1,128)} %copy-done.1, bf16[1024,256]{1,0:T(8,128)(2,1)} %get-tuple-element.17.hidden_ref, f32[1024,256]{1,0:T(8,128)} %get-tuple-element.18.mix_ref, ...), custom_call_target="tpu_custom_call" | custom-call | tf_op jit(solution)/shard_map/lower_backward/pallas_call | solution.py:737
  121.8 1.1 slice.51
  122.9 3.8 %all-to-all-start.3 = ((bf16[8,4,80,128]{3,2,1,0:T(8,128)(2,1)}), bf16[8,4,80,128]{3,2,1,0:T(8,128)(2,1)S(1)}, u32[]{:S(2)}, u32[]{:S(2)}) async-start(bf16[8,4,80,128]{3,2,1,0:T(8,128)(2,1)} %get-tuple-element.22), calls=%async_computation.3 | async-start | bytes 1310720 | tf_op jit(solution)/shard_map/all_to_all | solution.py:204
  126.8 2.1 %collective-permute-start.7 = (bf16[2,4,80,128]{3,2,1,0:T(8,128)(2,1)S(1)}, bf16[2,4,80,128]{3,2,1,0:T(8,128)(2,1)S(1)}, u32[]{:S(2)}, u32[]{:S(2)}) collective-permute-start(bf16[2,4,80,128]{3,2,1,0:T(8,128)(2,1)S(1)} %slice.119), channel_id=1, source_target_pairs={{0,2},{1,3},{2,0},{3,1},{4,6},{5,7},{6,4},{7,5},{8,10},{9,11},{10,... | collective-permute-start | bytes 491528 | tf_op jit(solution)/shard_map/ppermute | solution.py:214
  128.9 11.5 %collective-permute-done.7 = bf16[2,4,80,128]{3,2,1,0:T(8,128)(2,1)S(1)} collective-permute-done((bf16[2,4,80,128]{3,2,1,0:T(8,128)(2,1)S(1)}, bf16[2,4,80,128]{3,2,1,0:T(8,128)(2,1)S(1)}, u32[]{:S(2)}, u32[]{:S(2)}) %collective-permute-start.7) | collective-permute-done | bytes 163872 | tf_op jit(solution)/shard_map/ppermute | solution.py:214
  140.5 1.5 collective-permute-start.8
  142.1 2.9 %collective-permute-done.8 = bf16[1,4,80,128]{3,2,1,0:T(8,128)(2,1)S(1)} collective-permute-done((bf16[1,4,80,128]{3,2,1,0:T(8,128)(2,1)S(1)}, bf16[1,4,80,128]{3,2,1,0:T(8,128)(2,1)S(1)}, u32[]{:S(2)}, u32[]{:S(2)}) %collective-permute-start.8) | collective-permute-done | bytes 81952 | tf_op jit(solution)/shard_map/ppermute | solution.py:214
  145.8 1.9 collective-permute-start.11
  149.2 2.4 %collective-permute-done.11 = bf16[2,80,128]{2,1,0:T(8,128)(2,1)S(1)} collective-permute-done((bf16[2,80,128]{2,1,0:T(8,128)(2,1)S(1)}, bf16[2,80,128]{2,1,0:T(8,128)(2,1)S(1)}, u32[]{:S(2)}, u32[]{:S(2)}) %collective-permute-start.11) | collective-permute-done | bytes 40992 | tf_op jit(solution)/shard_map/ppermute | solution.py:214
  152.6 1.6 collective-permute-start.12
  154.2 2.6 %all-to-all-start.2 = ((bf16[32,64,256]{2,1,0:T(8,128)(2,1)}), bf16[32,64,256]{2,1,0:T(8,128)(2,1)S(1)}, u32[]{:S(2)}, u32[]{:S(2)}) async-start(bf16[32,64,256]{2,1,0:T(8,128)(2,1)} %bitcast.140), calls=%async_computation.2 | async-start | bytes 2097152 | tf_op jit(solution)/shard_map/all_to_all | solution.py:204
  156.9 1.8 collective-permute-start.13
  158.7 9.7 %collective-permute-done.13 = bf16[2,2,80,128]{3,2,1,0:T(8,128)(2,1)S(1)} collective-permute-done((bf16[2,2,80,128]{3,2,1,0:T(8,128)(2,1)S(1)}, bf16[2,2,80,128]{3,2,1,0:T(8,128)(2,1)S(1)}, u32[]{:S(2)}, u32[]{:S(2)}) %collective-permute-start.13) | collective-permute-done | bytes 81952 | tf_op jit(solution)/shard_map/ppermute | solution.py:214
  168.5 1.4 collective-permute-done.14
  171.9 11.1 %all-to-all-done.2 = bf16[32,64,256]{2,1,0:T(8,128)(2,1)S(1)} async-done(((bf16[32,64,256]{2,1,0:T(8,128)(2,1)}), bf16[32,64,256]{2,1,0:T(8,128)(2,1)S(1)}, u32[]{:S(2)}, u32[]{:S(2)}) %all-to-all-start.2) | async-done | bytes 1048608 | tf_op jit(solution)/shard_map/all_to_all | solution.py:204
  184.0 8.4 %update_table.1 = f32[4096,256]{1,0:T(8,128)} custom-call(s32[1,2048]{1,0:T(1,128)} %get-tuple-element.14.request_ref, s32[4,8,128]{2,1,0:T(8,128)} %bitcast.145, bf16[2048,256]{1,0:T(8,128)(2,1)} %bitcast.135, f32[4096,256]{1,0:T(8,128)} %table_ref.3), custom_call_target="tpu_custom_call" | custom-call | tf_op jit(solution)/shard_map/update_table/pallas_call | solution.py:186
  (69 shorter events, 12.1 us)
Async XLA Ops:
  0.6 1.0 copy-start
  0.6 19.6 %copy-start.3 = (s32[1,1024]{1,0:T(1,128)S(1)}, s32[1,1024]{1,0:T(1,128)}, u32[]{:S(2)}) copy-start(s32[1,1024]{1,0:T(1,128)} %row_ref.1) | copy-start | bytes 12292
  0.7 19.6 %copy-start.2 = (s32[1,1024,1]{1,2,0:T(1,128)S(1)}, s32[1,1024,1]{1,2,0:T(1,128)}, u32[]{:S(2)}) copy-start(s32[1,1024,1]{1,2,0:T(1,128)} %param.8) | copy-start | bytes 12292
  1.6 5.7 %collective-permute-start.2 = (bf16[16,1280]{1,0:T(8,128)(2,1)S(1)}, bf16[16,1280]{1,0:T(8,128)(2,1)S(1)}, u32[]{:S(2)}, u32[]{:S(2)}) collective-permute-start(bf16[16,1280]{1,0:T(8,128)(2,1)S(1)} %pad_maximum_fusion.5), channel_id=1, source_target_pairs={{0,8},{8,0},{16,24},{24,16},{1,9},{9,1},{17,25},{25,17},{2,10},{10... | collective-permute-start | bytes 122888 | tf_op jit(solution)/shard_map/ppermute | solution.py:214
  4.7 5.7 %collective-permute-start.1 = (bf16[16,1280]{1,0:T(8,128)(2,1)S(1)}, bf16[16,1280]{1,0:T(8,128)(2,1)S(1)}, u32[]{:S(2)}, u32[]{:S(2)}) collective-permute-start(bf16[16,1280]{1,0:T(8,128)(2,1)S(1)} %pad_maximum_fusion.5), channel_id=1, source_target_pairs={{0,16},{8,24},{16,0},{24,8},{1,17},{9,25},{17,1},{25,9},{2,18},{10... | collective-permute-start | bytes 122888 | tf_op jit(solution)/shard_map/ppermute | solution.py:214
  7.3 5.8 %collective-permute-start = (bf16[16,1280]{1,0:T(8,128)(2,1)S(1)}, bf16[16,1280]{1,0:T(8,128)(2,1)S(1)}, u32[]{:S(2)}, u32[]{:S(2)}) collective-permute-start(bf16[16,1280]{1,0:T(8,128)(2,1)S(1)} %pad_maximum_fusion.5), channel_id=1, source_target_pairs={{0,24},{8,16},{16,8},{24,0},{1,25},{9,17},{17,9},{25,1},{2,26},{10... | collective-permute-start | bytes 122888 | tf_op jit(solution)/shard_map/ppermute | solution.py:214
  13.2 5.4 %collective-permute-start.3 = (bf16[1,4,16,1280]{3,2,1,0:T(8,128)(2,1)S(1)}, bf16[1,4,16,1280]{3,2,1,0:T(8,128)(2,1)S(1)}, u32[]{:S(2)}, u32[]{:S(2)}) collective-permute-start(bf16[1,4,16,1280]{3,2,1,0:T(8,128)(2,1)S(1)} %maximum_bitcast_fusion.1), channel_id=1, source_target_pairs={{0,4},{1,5},{2,6},{3,7},{4,0},{5,1},{6,2},{7,3},{8,12},{9,13},{10,... | collective-permute-start | bytes 491528 | tf_op jit(solution)/shard_map/ppermute | solution.py:214
  18.7 24.5 %collective-permute-start.4 = (bf16[2,4,16,1280]{3,2,1,0:T(8,128)(2,1)S(1)}, bf16[2,4,16,1280]{3,2,1,0:T(8,128)(2,1)}, u32[]{:S(2)}, u32[]{:S(2)}) collective-permute-start(bf16[2,4,16,1280]{3,2,1,0:T(8,128)(2,1)S(1)} %maximum_bitcast_fusion), channel_id=1, source_target_pairs={{0,2},{1,3},{2,0},{3,1},{4,6},{5,7},{6,4},{7,5},{8,10},{9,11},{10,... | collective-permute-start | bytes 983048 | tf_op jit(solution)/shard_map/ppermute | solution.py:214
  21.2 0.6 copy-start.1
  21.8 9.7 %all-to-all-start = ((s32[32,1,64]{2,1,0:T(1,128)}), s32[32,1,64]{2,1,0:T(1,128)S(1)}, u32[]{:S(2)}, u32[]{:S(2)}) async-start(s32[32,1,64]{2,1,0:T(1,128)} %bitcast.2), calls=%async_computation | async-start | bytes 32768 | tf_op jit(solution)/shard_map/all_to_all | solution.py:204
  31.5 0.6 copy-start.7
  40.3 28.8 %all-to-all-start.1 = ((bf16[32,64,256]{2,1,0:T(8,128)(2,1)}), bf16[32,64,256]{2,1,0:T(8,128)(2,1)S(1)}, u32[]{:S(2)}, u32[]{:S(2)}) async-start(bf16[32,64,256]{2,1,0:T(8,128)(2,1)} %bitcast.141), calls=%async_computation.1 | async-start | bytes 2097152 | tf_op jit(solution)/shard_map/all_to_all | solution.py:204
  44.3 2.2 %collective-permute-start.5 = (bf16[4,4,16,1280]{3,2,1,0:T(8,128)(2,1)S(1)}, bf16[4,4,16,1280]{3,2,1,0:T(8,128)(2,1)S(1)}, u32[]{:S(2)}, u32[]{:S(2)}) collective-permute-start(bf16[4,4,16,1280]{3,2,1,0:T(8,128)(2,1)S(1)} %bitcast.136), channel_id=1, source_target_pairs={{0,1},{1,0},{2,3},{3,2},{4,5},{5,4},{6,7},{7,6},{8,9},{9,8},{10,11... | collective-permute-start | bytes 1966088 | tf_op jit(solution)/shard_map/ppermute | solution.py:214
  69.2 1.0 copy-start.4
  121.8 5.0 %copy-start.6 = (bf16[8,4,80,128]{3,2,1,0:T(8,128)(2,1)S(1)}, bf16[8,4,80,128]{3,2,1,0:T(8,128)(2,1)}, u32[]{:S(2)}) copy-start(bf16[8,4,80,128]{3,2,1,0:T(8,128)(2,1)} %get-tuple-element.21) | copy-start | bytes 1966084
  122.8 3.9 %collective-permute-start.6 = (bf16[4,4,80,128]{3,2,1,0:T(8,128)(2,1)S(1)}, bf16[4,4,80,128]{3,2,1,0:T(8,128)(2,1)S(1)}, u32[]{:S(2)}, u32[]{:S(2)}) collective-permute-start(bf16[4,4,80,128]{3,2,1,0:T(8,128)(2,1)S(1)} %slice.51), channel_id=1, source_target_pairs={{0,1},{1,0},{2,3},{3,2},{4,5},{5,4},{6,7},{7,6},{8,9},{9,8},{10,11... | collective-permute-start | bytes 983048 | tf_op jit(solution)/shard_map/ppermute | solution.py:214
  122.9 19.1 %all-to-all-start.3 = ((bf16[8,4,80,128]{3,2,1,0:T(8,128)(2,1)}), bf16[8,4,80,128]{3,2,1,0:T(8,128)(2,1)S(1)}, u32[]{:S(2)}, u32[]{:S(2)}) async-start(bf16[8,4,80,128]{3,2,1,0:T(8,128)(2,1)} %get-tuple-element.22), calls=%async_computation.3 | async-start | bytes 1310720 | tf_op jit(solution)/shard_map/all_to_all | solution.py:204
  126.8 13.6 %collective-permute-start.7 = (bf16[2,4,80,128]{3,2,1,0:T(8,128)(2,1)S(1)}, bf16[2,4,80,128]{3,2,1,0:T(8,128)(2,1)S(1)}, u32[]{:S(2)}, u32[]{:S(2)}) collective-permute-start(bf16[2,4,80,128]{3,2,1,0:T(8,128)(2,1)S(1)} %slice.119), channel_id=1, source_target_pairs={{0,2},{1,3},{2,0},{3,1},{4,6},{5,7},{6,4},{7,5},{8,10},{9,11},{10,... | collective-permute-start | bytes 491528 | tf_op jit(solution)/shard_map/ppermute | solution.py:214
  140.5 4.5 %collective-permute-start.8 = (bf16[1,4,80,128]{3,2,1,0:T(8,128)(2,1)S(1)}, bf16[1,4,80,128]{3,2,1,0:T(8,128)(2,1)S(1)}, u32[]{:S(2)}, u32[]{:S(2)}) collective-permute-start(bf16[1,4,80,128]{3,2,1,0:T(8,128)(2,1)S(1)} %slice.120), channel_id=1, source_target_pairs={{0,4},{1,5},{2,6},{3,7},{4,0},{5,1},{6,2},{7,3},{8,12},{9,13},{10,... | collective-permute-start | bytes 245768 | tf_op jit(solution)/shard_map/ppermute | solution.py:214
  145.1 4.1 %collective-permute-start.9 = (bf16[2,80,128]{2,1,0:T(8,128)(2,1)S(1)}, bf16[2,80,128]{2,1,0:T(8,128)(2,1)S(1)}, u32[]{:S(2)}, u32[]{:S(2)}) collective-permute-start(bf16[2,80,128]{2,1,0:T(8,128)(2,1)S(1)} %get-tuple-element.35), channel_id=1, source_target_pairs={{0,8},{8,0},{16,24},{24,16},{1,9},{9,1},{17,25},{25,17},{2,10},{10... | collective-permute-start | bytes 122888 | tf_op jit(solution)/shard_map/ppermute | solution.py:214
  145.8 5.8 %collective-permute-start.11 = (bf16[2,80,128]{2,1,0:T(8,128)(2,1)S(1)}, bf16[2,80,128]{2,1,0:T(8,128)(2,1)S(1)}, u32[]{:S(2)}, u32[]{:S(2)}) collective-permute-start(bf16[2,80,128]{2,1,0:T(8,128)(2,1)S(1)} %get-tuple-element.36), channel_id=1, source_target_pairs={{0,24},{8,16},{16,8},{24,0},{1,25},{9,17},{17,9},{25,1},{2,26},{10... | collective-permute-start | bytes 122888 | tf_op jit(solution)/shard_map/ppermute | solution.py:214
  147.7 4.9 %collective-permute-start.10 = (bf16[2,80,128]{2,1,0:T(8,128)(2,1)S(1)}, bf16[2,80,128]{2,1,0:T(8,128)(2,1)S(1)}, u32[]{:S(2)}, u32[]{:S(2)}) collective-permute-start(bf16[2,80,128]{2,1,0:T(8,128)(2,1)S(1)} %get-tuple-element.37), channel_id=1, source_target_pairs={{0,16},{8,24},{16,0},{24,8},{1,17},{9,25},{17,1},{25,9},{2,18},{10... | collective-permute-start | bytes 122888 | tf_op jit(solution)/shard_map/ppermute | solution.py:214
  152.6 4.2 %collective-permute-start.12 = (bf16[1,2,80,128]{3,2,1,0:T(8,128)(2,1)S(1)}, bf16[1,2,80,128]{3,2,1,0:T(8,128)(2,1)S(1)}, u32[]{:S(2)}, u32[]{:S(2)}) collective-permute-start(bf16[1,2,80,128]{3,2,1,0:T(8,128)(2,1)S(1)} %fusion.9), channel_id=1, source_target_pairs={{0,4},{1,5},{2,6},{3,7},{4,0},{5,1},{6,2},{7,3},{8,12},{9,13},{10,... | collective-permute-start | bytes 122888 | tf_op jit(solution)/shard_map/ppermute | solution.py:214
  154.2 28.8 %all-to-all-start.2 = ((bf16[32,64,256]{2,1,0:T(8,128)(2,1)}), bf16[32,64,256]{2,1,0:T(8,128)(2,1)S(1)}, u32[]{:S(2)}, u32[]{:S(2)}) async-start(bf16[32,64,256]{2,1,0:T(8,128)(2,1)} %bitcast.140), calls=%async_computation.2 | async-start | bytes 2097152 | tf_op jit(solution)/shard_map/all_to_all | solution.py:204
  156.9 11.5 %collective-permute-start.13 = (bf16[2,2,80,128]{3,2,1,0:T(8,128)(2,1)S(1)}, bf16[2,2,80,128]{3,2,1,0:T(8,128)(2,1)S(1)}, u32[]{:S(2)}, u32[]{:S(2)}) collective-permute-start(bf16[2,2,80,128]{3,2,1,0:T(8,128)(2,1)S(1)} %maximum_bitcast_fusion.2), channel_id=1, source_target_pairs={{0,2},{1,3},{2,0},{3,1},{4,6},{5,7},{6,4},{7,5},{8,10},{9,11},{10,... | collective-permute-start | bytes 245768 | tf_op jit(solution)/shard_map/ppermute | solution.py:214
  168.4 1.5 collective-permute-start.14
  183.0 1.0 copy-start.5

commit v2 on v1

--- a/solution.py
+++ b/solution.py
@@ -68,7 +68,7 @@
             jax.ShapeDtypeStruct((1, length), jnp.int32),
             jax.ShapeDtypeStruct((owners, capacity), jnp.int32),
         ),
-        compiler_params=pltpu.CompilerParams(vmem_limit_bytes=8 << 20),
+        compiler_params=pltpu.CompilerParams(vmem_limit_bytes=62 << 20),
         name="slot_index",
     )(owner, offset)
 
@@ -195,7 +195,7 @@
         out_specs=pl.BlockSpec((block, width), lambda i: (i, 0)),
         out_shape=jax.ShapeDtypeStruct((rows, width), F32),
         scratch_shapes=[pltpu.VMEM((group, slots), BF16), pltpu.VMEM((16, slots), BF16)],
-        compiler_params=pltpu.CompilerParams(vmem_limit_bytes=62 << 20),
+        compiler_params=pltpu.CompilerParams(vmem_limit_bytes=60 << 20),
         name="update_table",
     )(requested, staleness.reshape(rows // block, block // 128, 128), incoming, table)
 
@@ -292,7 +292,8 @@
     total = planes[0]
     held = planes.astype(BF16)
     for flip in range(1, planes.shape[0]):
-        total = total + trade(held[flip], "fsdp", flip).astype(F32)
+        got = trade(held[flip], "fsdp", flip)
+        total = total + got.astype(F32)
     return spread_plane((total * scale).astype(BF16))
 
 

time: 193 us -> 193 us (level)
  no operation moved by 1% of the time
where the time goes in v2:
time: 193 us; the launch traced here: 192 us
  waiting for transfers between devices  79.9 us (41%)
  Pallas kernels  69.9 us (36%)
  starting transfers between devices  31.4 us (16%)
  local copies, waits for them, and re-layouts  6.29 us (3%)
  other arithmetic  4.02 us (2%)
    ppermute x15, waiting for transfers between devices, trade(): return lax.ppermute(payload, name, [(at, at ^ flip) for at in range(size)])  40.5 us
    all_to_all x4, waiting for transfers between devices, swap(): lax.all_to_all(payload, axes, split_axis=0, concat_axis=0, tiled=True)  39.4 us
    pallas_call x1, Pallas kernels, run_top(): pl.pallas_call(functools.partial(top_kernel, tuple(buffers), layers), in_...  31.6 us
    pallas_call x1, Pallas kernels, run_lower(): pl.pallas_call(functools.partial(lower_kernel, tuple(buffers), layer), in...  20 us
    ppermute x15, starting transfers between devices, trade(): return lax.ppermute(payload, name, [(at, at ^ flip) for at in range(size)])  19.6 us
    all_to_all x4, starting transfers between devices, swap(): lax.all_to_all(payload, axes, split_axis=0, concat_axis=0, tiled=True)  11.8 us
    pallas_call x1, Pallas kernels, update_table(): pl.pallas_call(update_kernel, grid=(rows // block,), in_specs=[pl.BlockSp...  8.38 us
    pallas_call x1, Pallas kernels, look_up(): pl.pallas_call(lookup_kernel, grid=(rows // some,), in_specs=[pl.BlockSpe...  8.22 us
  transfers between devices with their start and end apart: 19, of which 14 were waited for; matrix products, arithmetic and copies ran while one was open for 3% of the time, Pallas kernels for 5%

profile of v2, /device:TPU:0, one launch (start us, length us, event | category | flops | bytes accessed | tf_op | source)
XLA Modules:
  0.0 192.4 jit_solution(14466412577806333707)
XLA Ops:
  1.6 3.1 %collective-permute-start.2 = (bf16[16,1280]{1,0:T(8,128)(2,1)S(1)}, bf16[16,1280]{1,0:T(8,128)(2,1)S(1)}, u32[]{:S(2)}, u32[]{:S(2)}) collective-permute-start(bf16[16,1280]{1,0:T(8,128)(2,1)S(1)} %pad_maximum_fusion.5), channel_id=1, source_target_pairs={{0,8},{8,0},{16,24},{24,16},{1,9},{9,1},{17,25},{25,17},{2,10},{10... | collective-permute-start | bytes 122888 | tf_op jit(solution)/shard_map/ppermute | solution.py:214
  4.7 2.6 %collective-permute-start.1 = (bf16[16,1280]{1,0:T(8,128)(2,1)S(1)}, bf16[16,1280]{1,0:T(8,128)(2,1)S(1)}, u32[]{:S(2)}, u32[]{:S(2)}) collective-permute-start(bf16[16,1280]{1,0:T(8,128)(2,1)S(1)} %pad_maximum_fusion.5), channel_id=1, source_target_pairs={{0,16},{8,24},{16,0},{24,8},{1,17},{9,25},{17,1},{25,9},{2,18},{10... | collective-permute-start | bytes 122888 | tf_op jit(solution)/shard_map/ppermute | solution.py:214
  7.3 3.1 %collective-permute-done.1 = bf16[16,1280]{1,0:T(8,128)(2,1)S(1)} collective-permute-done((bf16[16,1280]{1,0:T(8,128)(2,1)S(1)}, bf16[16,1280]{1,0:T(8,128)(2,1)S(1)}, u32[]{:S(2)}, u32[]{:S(2)}) %collective-permute-start.1) | collective-permute-done | bytes 40992 | tf_op jit(solution)/shard_map/ppermute | solution.py:214
  10.4 2.7 %collective-permute-done = bf16[16,1280]{1,0:T(8,128)(2,1)S(1)} collective-permute-done((bf16[16,1280]{1,0:T(8,128)(2,1)S(1)}, bf16[16,1280]{1,0:T(8,128)(2,1)S(1)}, u32[]{:S(2)}, u32[]{:S(2)}) %collective-permute-start) | collective-permute-done | bytes 40992 | tf_op jit(solution)/shard_map/ppermute | solution.py:214
  13.2 1.6 collective-permute-start.3
  14.8 3.8 %collective-permute-done.3 = bf16[1,4,16,1280]{3,2,1,0:T(8,128)(2,1)S(1)} collective-permute-done((bf16[1,4,16,1280]{3,2,1,0:T(8,128)(2,1)S(1)}, bf16[1,4,16,1280]{3,2,1,0:T(8,128)(2,1)S(1)}, u32[]{:S(2)}, u32[]{:S(2)}) %collective-permute-start.3) | collective-permute-done | bytes 163872 | tf_op jit(solution)/shard_map/ppermute | solution.py:214
  18.7 1.6 collective-permute-start.4
  20.3 1.7 slot_index.1
  21.9 2.5 %all-to-all-start = ((s32[32,1,64]{2,1,0:T(1,128)}), s32[32,1,64]{2,1,0:T(1,128)S(1)}, u32[]{:S(2)}, u32[]{:S(2)}) async-start(s32[32,1,64]{2,1,0:T(1,128)} %bitcast.144), calls=%async_computation | async-start | bytes 32768 | tf_op jit(solution)/shard_map/all_to_all | solution.py:204
  24.5 7.1 %all-to-all-done = s32[32,1,64]{2,1,0:T(1,128)S(1)} async-done(((s32[32,1,64]{2,1,0:T(1,128)}), s32[32,1,64]{2,1,0:T(1,128)S(1)}, u32[]{:S(2)}, u32[]{:S(2)}) %all-to-all-start) | async-done | bytes 8224 | tf_op jit(solution)/shard_map/all_to_all | solution.py:204
  32.2 8.2 %look_up.1 = (bf16[2048,256]{1,0:T(8,128)(2,1)}, s32[1,2048]{1,0:T(1,128)}) custom-call(s32[32,64]{1,0:T(8,128)} %bitcast.142, f32[4096,256]{1,0:T(8,128)} %table_ref.3), custom_call_target="tpu_custom_call" | custom-call | tf_op jit(solution)/shard_map/look_up/pallas_call | solution.py:133
  40.4 2.8 %all-to-all-start.1 = ((bf16[32,64,256]{2,1,0:T(8,128)(2,1)}), bf16[32,64,256]{2,1,0:T(8,128)(2,1)S(1)}, u32[]{:S(2)}, u32[]{:S(2)}) async-start(bf16[32,64,256]{2,1,0:T(8,128)(2,1)} %bitcast.139), calls=%async_computation.1 | async-start | bytes 2097152 | tf_op jit(solution)/shard_map/all_to_all | solution.py:204
  45.1 1.5 collective-permute-done.5
  46.9 1.2 copy.46
  48.1 21.2 %all-to-all-done.1 = bf16[32,64,256]{2,1,0:T(8,128)(2,1)S(1)} async-done(((bf16[32,64,256]{2,1,0:T(8,128)(2,1)}), bf16[32,64,256]{2,1,0:T(8,128)(2,1)S(1)}, u32[]{:S(2)}, u32[]{:S(2)}) %all-to-all-start.1) | async-done | bytes 1048608 | tf_op jit(solution)/shard_map/all_to_all | solution.py:204
  70.3 31.6 %forward_and_last_backward.1 = (bf16[1024,256]{1,0:T(8,128)(2,1)}, bf16[1024,256]{1,0:T(8,128)(2,1)}, f32[1024,256]{1,0:T(8,128)}, f32[1024,256]{1,0:T(8,128)}, ...) custom-call(s32[2]{0:T(128)} %pad_add_fusion.here_ref, s32[1,1024]{1,0:T(1,128)} %get-tuple-element.15.target_ref, ...), custom_call_target="tpu_custom_call" | custom-call | tf_op jit(solution)/shard_map/forward_and_last_backward/pallas_call | solution.py:670
  101.8 20.0 %lower_backward.1 = (bf16[2048,256]{1,0:T(8,128)(2,1)}, bf16[8,4,80,128]{3,2,1,0:T(8,128)(2,1)}, bf16[8,128]{1,0:T(8,128)(2,1)}) custom-call(s32[2]{0:T(128)} %pad_add_fusion.here_ref, s32[1,1024]{1,0:T(1,128)} %get-tuple-element.15.target_ref, bf16[1024,256]{1,0:T(8,128)(2,1)} %get-tuple-element.17.hidden_ref, f32[1024,256]{1,0:T(8,128)} %get-tuple-element.18.mix_ref, ...), custom_call_target="tpu_custom_call" | custom-call | tf_op jit(solution)/shard_map/lower_backward/pallas_call | solution.py:738
  121.8 1.1 slice.51
  123.0 3.8 %all-to-all-start.3 = ((bf16[8,4,80,128]{3,2,1,0:T(8,128)(2,1)}), bf16[8,4,80,128]{3,2,1,0:T(8,128)(2,1)S(1)}, u32[]{:S(2)}, u32[]{:S(2)}) async-start(bf16[8,4,80,128]{3,2,1,0:T(8,128)(2,1)} %get-tuple-element.22), calls=%async_computation.3 | async-start | bytes 1310720 | tf_op jit(solution)/shard_map/all_to_all | solution.py:204
  126.9 2.1 %collective-permute-start.7 = (bf16[2,4,80,128]{3,2,1,0:T(8,128)(2,1)S(1)}, bf16[2,4,80,128]{3,2,1,0:T(8,128)(2,1)S(1)}, u32[]{:S(2)}, u32[]{:S(2)}) collective-permute-start(bf16[2,4,80,128]{3,2,1,0:T(8,128)(2,1)S(1)} %slice.119), channel_id=1, source_target_pairs={{0,2},{1,3},{2,0},{3,1},{4,6},{5,7},{6,4},{7,5},{8,10},{9,11},{10,... | collective-permute-start | bytes 491528 | tf_op jit(solution)/shard_map/ppermute | solution.py:214
  129.0 11.5 %collective-permute-done.7 = bf16[2,4,80,128]{3,2,1,0:T(8,128)(2,1)S(1)} collective-permute-done((bf16[2,4,80,128]{3,2,1,0:T(8,128)(2,1)S(1)}, bf16[2,4,80,128]{3,2,1,0:T(8,128)(2,1)S(1)}, u32[]{:S(2)}, u32[]{:S(2)}) %collective-permute-start.7) | collective-permute-done | bytes 163872 | tf_op jit(solution)/shard_map/ppermute | solution.py:214
  140.5 1.5 collective-permute-start.8
  142.2 2.9 %collective-permute-done.8 = bf16[1,4,80,128]{3,2,1,0:T(8,128)(2,1)S(1)} collective-permute-done((bf16[1,4,80,128]{3,2,1,0:T(8,128)(2,1)S(1)}, bf16[1,4,80,128]{3,2,1,0:T(8,128)(2,1)S(1)}, u32[]{:S(2)}, u32[]{:S(2)}) %collective-permute-start.8) | collective-permute-done | bytes 81952 | tf_op jit(solution)/shard_map/ppermute | solution.py:214
  145.8 1.9 collective-permute-start.11
  149.2 2.4 %collective-permute-done.11 = bf16[2,80,128]{2,1,0:T(8,128)(2,1)S(1)} collective-permute-done((bf16[2,80,128]{2,1,0:T(8,128)(2,1)S(1)}, bf16[2,80,128]{2,1,0:T(8,128)(2,1)S(1)}, u32[]{:S(2)}, u32[]{:S(2)}) %collective-permute-start.11) | collective-permute-done | bytes 40992 | tf_op jit(solution)/shard_map/ppermute | solution.py:214
  152.7 1.6 collective-permute-start.12
  154.2 2.6 %all-to-all-start.2 = ((bf16[32,64,256]{2,1,0:T(8,128)(2,1)}), bf16[32,64,256]{2,1,0:T(8,128)(2,1)S(1)}, u32[]{:S(2)}, u32[]{:S(2)}) async-start(bf16[32,64,256]{2,1,0:T(8,128)(2,1)} %bitcast.29), calls=%async_computation.2 | async-start | bytes 2097152 | tf_op jit(solution)/shard_map/all_to_all | solution.py:204
  156.9 1.8 collective-permute-start.13
  158.7 9.7 %collective-permute-done.13 = bf16[2,2,80,128]{3,2,1,0:T(8,128)(2,1)S(1)} collective-permute-done((bf16[2,2,80,128]{3,2,1,0:T(8,128)(2,1)S(1)}, bf16[2,2,80,128]{3,2,1,0:T(8,128)(2,1)S(1)}, u32[]{:S(2)}, u32[]{:S(2)}) %collective-permute-start.13) | collective-permute-done | bytes 81952 | tf_op jit(solution)/shard_map/ppermute | solution.py:214
  168.6 1.4 collective-permute-done.14
  172.0 11.1 %all-to-all-done.2 = bf16[32,64,256]{2,1,0:T(8,128)(2,1)S(1)} async-done(((bf16[32,64,256]{2,1,0:T(8,128)(2,1)}), bf16[32,64,256]{2,1,0:T(8,128)(2,1)S(1)}, u32[]{:S(2)}, u32[]{:S(2)}) %all-to-all-start.2) | async-done | bytes 1048608 | tf_op jit(solution)/shard_map/all_to_all | solution.py:204
  184.0 8.4 %update_table.1 = f32[4096,256]{1,0:T(8,128)} custom-call(s32[1,2048]{1,0:T(1,128)} %get-tuple-element.14.request_ref, s32[4,8,128]{2,1,0:T(8,128)} %bitcast.143, bf16[2048,256]{1,0:T(8,128)(2,1)} %bitcast.134, f32[4096,256]{1,0:T(8,128)} %table_ref.3), custom_call_target="tpu_custom_call" | custom-call | tf_op jit(solution)/shard_map/update_table/pallas_call | solution.py:186
  (63 shorter events, 11.5 us)
Async XLA Ops:
  0.6 1.0 copy-start
  1.6 5.7 %collective-permute-start.2 = (bf16[16,1280]{1,0:T(8,128)(2,1)S(1)}, bf16[16,1280]{1,0:T(8,128)(2,1)S(1)}, u32[]{:S(2)}, u32[]{:S(2)}) collective-permute-start(bf16[16,1280]{1,0:T(8,128)(2,1)S(1)} %pad_maximum_fusion.5), channel_id=1, source_target_pairs={{0,8},{8,0},{16,24},{24,16},{1,9},{9,1},{17,25},{25,17},{2,10},{10... | collective-permute-start | bytes 122888 | tf_op jit(solution)/shard_map/ppermute | solution.py:214
  4.7 5.7 %collective-permute-start.1 = (bf16[16,1280]{1,0:T(8,128)(2,1)S(1)}, bf16[16,1280]{1,0:T(8,128)(2,1)S(1)}, u32[]{:S(2)}, u32[]{:S(2)}) collective-permute-start(bf16[16,1280]{1,0:T(8,128)(2,1)S(1)} %pad_maximum_fusion.5), channel_id=1, source_target_pairs={{0,16},{8,24},{16,0},{24,8},{1,17},{9,25},{17,1},{25,9},{2,18},{10... | collective-permute-start | bytes 122888 | tf_op jit(solution)/shard_map/ppermute | solution.py:214
  7.3 5.8 %collective-permute-start = (bf16[16,1280]{1,0:T(8,128)(2,1)S(1)}, bf16[16,1280]{1,0:T(8,128)(2,1)S(1)}, u32[]{:S(2)}, u32[]{:S(2)}) collective-permute-start(bf16[16,1280]{1,0:T(8,128)(2,1)S(1)} %pad_maximum_fusion.5), channel_id=1, source_target_pairs={{0,24},{8,16},{16,8},{24,0},{1,25},{9,17},{17,9},{25,1},{2,26},{10... | collective-permute-start | bytes 122888 | tf_op jit(solution)/shard_map/ppermute | solution.py:214
  13.2 5.4 %collective-permute-start.3 = (bf16[1,4,16,1280]{3,2,1,0:T(8,128)(2,1)S(1)}, bf16[1,4,16,1280]{3,2,1,0:T(8,128)(2,1)S(1)}, u32[]{:S(2)}, u32[]{:S(2)}) collective-permute-start(bf16[1,4,16,1280]{3,2,1,0:T(8,128)(2,1)S(1)} %maximum_bitcast_fusion.1), channel_id=1, source_target_pairs={{0,4},{1,5},{2,6},{3,7},{4,0},{5,1},{6,2},{7,3},{8,12},{9,13},{10,... | collective-permute-start | bytes 491528 | tf_op jit(solution)/shard_map/ppermute | solution.py:214
  18.7 24.6 %collective-permute-start.4 = (bf16[2,4,16,1280]{3,2,1,0:T(8,128)(2,1)S(1)}, bf16[2,4,16,1280]{3,2,1,0:T(8,128)(2,1)}, u32[]{:S(2)}, u32[]{:S(2)}) collective-permute-start(bf16[2,4,16,1280]{3,2,1,0:T(8,128)(2,1)S(1)} %maximum_bitcast_fusion), channel_id=1, source_target_pairs={{0,2},{1,3},{2,0},{3,1},{4,6},{5,7},{6,4},{7,5},{8,10},{9,11},{10,... | collective-permute-start | bytes 983048 | tf_op jit(solution)/shard_map/ppermute | solution.py:214
  21.9 9.7 %all-to-all-start = ((s32[32,1,64]{2,1,0:T(1,128)}), s32[32,1,64]{2,1,0:T(1,128)S(1)}, u32[]{:S(2)}, u32[]{:S(2)}) async-start(s32[32,1,64]{2,1,0:T(1,128)} %bitcast.144), calls=%async_computation | async-start | bytes 32768 | tf_op jit(solution)/shard_map/all_to_all | solution.py:204
  31.6 0.6 copy-start.4
  40.4 28.8 %all-to-all-start.1 = ((bf16[32,64,256]{2,1,0:T(8,128)(2,1)}), bf16[32,64,256]{2,1,0:T(8,128)(2,1)S(1)}, u32[]{:S(2)}, u32[]{:S(2)}) async-start(bf16[32,64,256]{2,1,0:T(8,128)(2,1)} %bitcast.139), calls=%async_computation.1 | async-start | bytes 2097152 | tf_op jit(solution)/shard_map/all_to_all | solution.py:204
  44.4 2.2 %collective-permute-start.5 = (bf16[4,4,16,1280]{3,2,1,0:T(8,128)(2,1)S(1)}, bf16[4,4,16,1280]{3,2,1,0:T(8,128)(2,1)S(1)}, u32[]{:S(2)}, u32[]{:S(2)}) collective-permute-start(bf16[4,4,16,1280]{3,2,1,0:T(8,128)(2,1)S(1)} %bitcast.135), channel_id=1, source_target_pairs={{0,1},{1,0},{2,3},{3,2},{4,5},{5,4},{6,7},{7,6},{8,9},{9,8},{10,11... | collective-permute-start | bytes 1966088 | tf_op jit(solution)/shard_map/ppermute | solution.py:214
  69.3 1.0 copy-start.1
  121.8 4.9 %copy-start.3 = (bf16[8,4,80,128]{3,2,1,0:T(8,128)(2,1)S(1)}, bf16[8,4,80,128]{3,2,1,0:T(8,128)(2,1)}, u32[]{:S(2)}) copy-start(bf16[8,4,80,128]{3,2,1,0:T(8,128)(2,1)} %get-tuple-element.21) | copy-start | bytes 1966084
  122.9 3.9 %collective-permute-start.6 = (bf16[4,4,80,128]{3,2,1,0:T(8,128)(2,1)S(1)}, bf16[4,4,80,128]{3,2,1,0:T(8,128)(2,1)S(1)}, u32[]{:S(2)}, u32[]{:S(2)}) collective-permute-start(bf16[4,4,80,128]{3,2,1,0:T(8,128)(2,1)S(1)} %slice.51), channel_id=1, source_target_pairs={{0,1},{1,0},{2,3},{3,2},{4,5},{5,4},{6,7},{7,6},{8,9},{9,8},{10,11... | collective-permute-start | bytes 983048 | tf_op jit(solution)/shard_map/ppermute | solution.py:214
  123.0 19.1 %all-to-all-start.3 = ((bf16[8,4,80,128]{3,2,1,0:T(8,128)(2,1)}), bf16[8,4,80,128]{3,2,1,0:T(8,128)(2,1)S(1)}, u32[]{:S(2)}, u32[]{:S(2)}) async-start(bf16[8,4,80,128]{3,2,1,0:T(8,128)(2,1)} %get-tuple-element.22), calls=%async_computation.3 | async-start | bytes 1310720 | tf_op jit(solution)/shard_map/all_to_all | solution.py:204
  126.9 13.6 %collective-permute-start.7 = (bf16[2,4,80,128]{3,2,1,0:T(8,128)(2,1)S(1)}, bf16[2,4,80,128]{3,2,1,0:T(8,128)(2,1)S(1)}, u32[]{:S(2)}, u32[]{:S(2)}) collective-permute-start(bf16[2,4,80,128]{3,2,1,0:T(8,128)(2,1)S(1)} %slice.119), channel_id=1, source_target_pairs={{0,2},{1,3},{2,0},{3,1},{4,6},{5,7},{6,4},{7,5},{8,10},{9,11},{10,... | collective-permute-start | bytes 491528 | tf_op jit(solution)/shard_map/ppermute | solution.py:214
  140.5 4.5 %collective-permute-start.8 = (bf16[1,4,80,128]{3,2,1,0:T(8,128)(2,1)S(1)}, bf16[1,4,80,128]{3,2,1,0:T(8,128)(2,1)S(1)}, u32[]{:S(2)}, u32[]{:S(2)}) collective-permute-start(bf16[1,4,80,128]{3,2,1,0:T(8,128)(2,1)S(1)} %slice.120), channel_id=1, source_target_pairs={{0,4},{1,5},{2,6},{3,7},{4,0},{5,1},{6,2},{7,3},{8,12},{9,13},{10,... | collective-permute-start | bytes 245768 | tf_op jit(solution)/shard_map/ppermute | solution.py:214
  145.1 4.1 %collective-permute-start.9 = (bf16[2,80,128]{2,1,0:T(8,128)(2,1)S(1)}, bf16[2,80,128]{2,1,0:T(8,128)(2,1)S(1)}, u32[]{:S(2)}, u32[]{:S(2)}) collective-permute-start(bf16[2,80,128]{2,1,0:T(8,128)(2,1)S(1)} %get-tuple-element.35), channel_id=1, source_target_pairs={{0,8},{8,0},{16,24},{24,16},{1,9},{9,1},{17,25},{25,17},{2,10},{10... | collective-permute-start | bytes 122888 | tf_op jit(solution)/shard_map/ppermute | solution.py:214
  145.8 5.8 %collective-permute-start.11 = (bf16[2,80,128]{2,1,0:T(8,128)(2,1)S(1)}, bf16[2,80,128]{2,1,0:T(8,128)(2,1)S(1)}, u32[]{:S(2)}, u32[]{:S(2)}) collective-permute-start(bf16[2,80,128]{2,1,0:T(8,128)(2,1)S(1)} %get-tuple-element.36), channel_id=1, source_target_pairs={{0,24},{8,16},{16,8},{24,0},{1,25},{9,17},{17,9},{25,1},{2,26},{10... | collective-permute-start | bytes 122888 | tf_op jit(solution)/shard_map/ppermute | solution.py:214
  147.7 4.9 %collective-permute-start.10 = (bf16[2,80,128]{2,1,0:T(8,128)(2,1)S(1)}, bf16[2,80,128]{2,1,0:T(8,128)(2,1)S(1)}, u32[]{:S(2)}, u32[]{:S(2)}) collective-permute-start(bf16[2,80,128]{2,1,0:T(8,128)(2,1)S(1)} %get-tuple-element.37), channel_id=1, source_target_pairs={{0,16},{8,24},{16,0},{24,8},{1,17},{9,25},{17,1},{25,9},{2,18},{10... | collective-permute-start | bytes 122888 | tf_op jit(solution)/shard_map/ppermute | solution.py:214
  152.7 4.2 %collective-permute-start.12 = (bf16[1,2,80,128]{3,2,1,0:T(8,128)(2,1)S(1)}, bf16[1,2,80,128]{3,2,1,0:T(8,128)(2,1)S(1)}, u32[]{:S(2)}, u32[]{:S(2)}) collective-permute-start(bf16[1,2,80,128]{3,2,1,0:T(8,128)(2,1)S(1)} %fusion.9), channel_id=1, source_target_pairs={{0,4},{1,5},{2,6},{3,7},{4,0},{5,1},{6,2},{7,3},{8,12},{9,13},{10,... | collective-permute-start | bytes 122888 | tf_op jit(solution)/shard_map/ppermute | solution.py:214
  154.2 28.8 %all-to-all-start.2 = ((bf16[32,64,256]{2,1,0:T(8,128)(2,1)}), bf16[32,64,256]{2,1,0:T(8,128)(2,1)S(1)}, u32[]{:S(2)}, u32[]{:S(2)}) async-start(bf16[32,64,256]{2,1,0:T(8,128)(2,1)} %bitcast.29), calls=%async_computation.2 | async-start | bytes 2097152 | tf_op jit(solution)/shard_map/all_to_all | solution.py:204
  156.9 11.5 %collective-permute-start.13 = (bf16[2,2,80,128]{3,2,1,0:T(8,128)(2,1)S(1)}, bf16[2,2,80,128]{3,2,1,0:T(8,128)(2,1)S(1)}, u32[]{:S(2)}, u32[]{:S(2)}) collective-permute-start(bf16[2,2,80,128]{3,2,1,0:T(8,128)(2,1)S(1)} %maximum_bitcast_fusion.2), channel_id=1, source_target_pairs={{0,2},{1,3},{2,0},{3,1},{4,6},{5,7},{6,4},{7,5},{8,10},{9,11},{10,... | collective-permute-start | bytes 245768 | tf_op jit(solution)/shard_map/ppermute | solution.py:214
  168.5 1.5 collective-permute-start.14
  183.1 1.0 copy-start.2

commit v3 on v2

--- a/solution.py
+++ b/solution.py
@@ -129,7 +129,7 @@
     owners, capacity = requested.shape
     rows, width = table.shape
     slots = owners * capacity
-    some = rows // 4
+    some = rows // 2
     return pl.pallas_call(
         lookup_kernel,
         grid=(rows // some,),
@@ -530,7 +530,7 @@
                 ]
         return carry
 
-    lax.fori_loop(0, 4 * width // BLOCK, weigh, 0)
+    each_block(4 * width // BLOCK, weigh)
 
 
 def peer_slot(peer, peers, here, flip):
@@ -653,7 +653,7 @@
         out_ref[...] += nn_dot(jnp.concatenate(hot, axis=1), chunk).astype(BF16)
         return carry
 
-    lax.fori_loop(0, rows_ref.shape[0] // (2 * lanes), step, 0)
+    each_block(rows_ref.shape[0] // (2 * lanes), step)
 
 
 def in_memory(count):

time: 193 us -> 192 us (level)
  no operation moved by 1% of the time
where the time goes in v3:
time: 192 us; the launch traced here: 191 us
  waiting for transfers between devices  80 us (42%)
  Pallas kernels  68.6 us (36%)
  starting transfers between devices  31.3 us (16%)
  local copies, waits for them, and re-layouts  6.29 us (3%)
  other arithmetic  4.02 us (2%)
    ppermute x15, waiting for transfers between devices, trade(): return lax.ppermute(payload, name, [(at, at ^ flip) for at in range(size)])  40.5 us
    all_to_all x4, waiting for transfers between devices, swap(): lax.all_to_all(payload, axes, split_axis=0, concat_axis=0, tiled=True)  39.4 us
    pallas_call x1, Pallas kernels, run_top(): pl.pallas_call(functools.partial(top_kernel, tuple(buffers), layers), in_...  30.5 us
    pallas_call x1, Pallas kernels, run_lower(): pl.pallas_call(functools.partial(lower_kernel, tuple(buffers), layer), in...  19.7 us
    ppermute x15, starting transfers between devices, trade(): return lax.ppermute(payload, name, [(at, at ^ flip) for at in range(size)])  19.5 us
    all_to_all x4, starting transfers between devices, swap(): lax.all_to_all(payload, axes, split_axis=0, concat_axis=0, tiled=True)  11.8 us
    pallas_call x1, Pallas kernels, update_table(): pl.pallas_call(update_kernel, grid=(rows // block,), in_specs=[pl.BlockSp...  8.38 us
    pallas_call x1, Pallas kernels, look_up(): pl.pallas_call(lookup_kernel, grid=(rows // some,), in_specs=[pl.BlockSpe...  8.34 us
  transfers between devices with their start and end apart: 19, of which 14 were waited for; matrix products, arithmetic and copies ran while one was open for 3% of the time, Pallas kernels for 5%

profile of v3, /device:TPU:0, one launch (start us, length us, event | category | flops | bytes accessed | tf_op | source)
XLA Modules:
  0.0 191.1 jit_solution(6604223206454946645)
XLA Ops:
  1.6 3.1 %collective-permute-start.2 = (bf16[16,1280]{1,0:T(8,128)(2,1)S(1)}, bf16[16,1280]{1,0:T(8,128)(2,1)S(1)}, u32[]{:S(2)}, u32[]{:S(2)}) collective-permute-start(bf16[16,1280]{1,0:T(8,128)(2,1)S(1)} %pad_maximum_fusion.5), channel_id=1, source_target_pairs={{0,8},{8,0},{16,24},{24,16},{1,9},{9,1},{17,25},{25,17},{2,10},{10... | collective-permute-start | bytes 122888 | tf_op jit(solution)/shard_map/ppermute | solution.py:214
  4.7 2.6 %collective-permute-start.1 = (bf16[16,1280]{1,0:T(8,128)(2,1)S(1)}, bf16[16,1280]{1,0:T(8,128)(2,1)S(1)}, u32[]{:S(2)}, u32[]{:S(2)}) collective-permute-start(bf16[16,1280]{1,0:T(8,128)(2,1)S(1)} %pad_maximum_fusion.5), channel_id=1, source_target_pairs={{0,16},{8,24},{16,0},{24,8},{1,17},{9,25},{17,1},{25,9},{2,18},{10... | collective-permute-start | bytes 122888 | tf_op jit(solution)/shard_map/ppermute | solution.py:214
  7.3 3.1 %collective-permute-done.1 = bf16[16,1280]{1,0:T(8,128)(2,1)S(1)} collective-permute-done((bf16[16,1280]{1,0:T(8,128)(2,1)S(1)}, bf16[16,1280]{1,0:T(8,128)(2,1)S(1)}, u32[]{:S(2)}, u32[]{:S(2)}) %collective-permute-start.1) | collective-permute-done | bytes 40992 | tf_op jit(solution)/shard_map/ppermute | solution.py:214
  10.4 2.7 %collective-permute-done = bf16[16,1280]{1,0:T(8,128)(2,1)S(1)} collective-permute-done((bf16[16,1280]{1,0:T(8,128)(2,1)S(1)}, bf16[16,1280]{1,0:T(8,128)(2,1)S(1)}, u32[]{:S(2)}, u32[]{:S(2)}) %collective-permute-start) | collective-permute-done | bytes 40992 | tf_op jit(solution)/shard_map/ppermute | solution.py:214
  13.2 1.6 collective-permute-start.3
  14.8 3.8 %collective-permute-done.3 = bf16[1,4,16,1280]{3,2,1,0:T(8,128)(2,1)S(1)} collective-permute-done((bf16[1,4,16,1280]{3,2,1,0:T(8,128)(2,1)S(1)}, bf16[1,4,16,1280]{3,2,1,0:T(8,128)(2,1)S(1)}, u32[]{:S(2)}, u32[]{:S(2)}) %collective-permute-start.3) | collective-permute-done | bytes 163872 | tf_op jit(solution)/shard_map/ppermute | solution.py:214
  18.7 1.6 collective-permute-start.4
  20.3 1.7 slot_index.1
  21.9 2.5 %all-to-all-start = ((s32[32,1,64]{2,1,0:T(1,128)}), s32[32,1,64]{2,1,0:T(1,128)S(1)}, u32[]{:S(2)}, u32[]{:S(2)}) async-start(s32[32,1,64]{2,1,0:T(1,128)} %bitcast.144), calls=%async_computation | async-start | bytes 32768 | tf_op jit(solution)/shard_map/all_to_all | solution.py:204
  24.5 7.1 %all-to-all-done = s32[32,1,64]{2,1,0:T(1,128)S(1)} async-done(((s32[32,1,64]{2,1,0:T(1,128)}), s32[32,1,64]{2,1,0:T(1,128)S(1)}, u32[]{:S(2)}, u32[]{:S(2)}) %all-to-all-start) | async-done | bytes 8224 | tf_op jit(solution)/shard_map/all_to_all | solution.py:204
  32.2 8.3 %look_up.1 = (bf16[2048,256]{1,0:T(8,128)(2,1)}, s32[1,2048]{1,0:T(1,128)}) custom-call(s32[32,64]{1,0:T(8,128)} %bitcast.142, f32[4096,256]{1,0:T(8,128)} %table_ref.3), custom_call_target="tpu_custom_call" | custom-call | tf_op jit(solution)/shard_map/look_up/pallas_call | solution.py:133
  40.6 2.8 %all-to-all-start.1 = ((bf16[32,64,256]{2,1,0:T(8,128)(2,1)}), bf16[32,64,256]{2,1,0:T(8,128)(2,1)S(1)}, u32[]{:S(2)}, u32[]{:S(2)}) async-start(bf16[32,64,256]{2,1,0:T(8,128)(2,1)} %bitcast.139), calls=%async_computation.1 | async-start | bytes 2097152 | tf_op jit(solution)/shard_map/all_to_all | solution.py:204
  45.2 1.5 collective-permute-done.5
  47.0 1.2 copy.46
  48.2 21.2 %all-to-all-done.1 = bf16[32,64,256]{2,1,0:T(8,128)(2,1)S(1)} async-done(((bf16[32,64,256]{2,1,0:T(8,128)(2,1)}), bf16[32,64,256]{2,1,0:T(8,128)(2,1)S(1)}, u32[]{:S(2)}, u32[]{:S(2)}) %all-to-all-start.1) | async-done | bytes 1048608 | tf_op jit(solution)/shard_map/all_to_all | solution.py:204
  70.4 30.5 %forward_and_last_backward.1 = (bf16[1024,256]{1,0:T(8,128)(2,1)}, bf16[1024,256]{1,0:T(8,128)(2,1)}, f32[1024,256]{1,0:T(8,128)}, f32[1024,256]{1,0:T(8,128)}, ...) custom-call(s32[2]{0:T(128)} %pad_add_fusion.here_ref, s32[1,1024]{1,0:T(1,128)} %get-tuple-element.15.target_ref, ...), custom_call_target="tpu_custom_call" | custom-call | tf_op jit(solution)/shard_map/forward_and_last_backward/pallas_call | solution.py:670
  100.8 19.7 %lower_backward.1 = (bf16[2048,256]{1,0:T(8,128)(2,1)}, bf16[8,4,80,128]{3,2,1,0:T(8,128)(2,1)}, bf16[8,128]{1,0:T(8,128)(2,1)}) custom-call(s32[2]{0:T(128)} %pad_add_fusion.here_ref, s32[1,1024]{1,0:T(1,128)} %get-tuple-element.15.target_ref, bf16[1024,256]{1,0:T(8,128)(2,1)} %get-tuple-element.17.hidden_ref, f32[1024,256]{1,0:T(8,128)} %get-tuple-element.18.mix_ref, ...), custom_call_target="tpu_custom_call" | custom-call | tf_op jit(solution)/shard_map/lower_backward/pallas_call | solution.py:738
  120.5 1.1 slice.51
  121.7 3.8 %all-to-all-start.3 = ((bf16[8,4,80,128]{3,2,1,0:T(8,128)(2,1)}), bf16[8,4,80,128]{3,2,1,0:T(8,128)(2,1)S(1)}, u32[]{:S(2)}, u32[]{:S(2)}) async-start(bf16[8,4,80,128]{3,2,1,0:T(8,128)(2,1)} %get-tuple-element.22), calls=%async_computation.3 | async-start | bytes 1310720 | tf_op jit(solution)/shard_map/all_to_all | solution.py:204
  125.6 2.1 %collective-permute-start.7 = (bf16[2,4,80,128]{3,2,1,0:T(8,128)(2,1)S(1)}, bf16[2,4,80,128]{3,2,1,0:T(8,128)(2,1)S(1)}, u32[]{:S(2)}, u32[]{:S(2)}) collective-permute-start(bf16[2,4,80,128]{3,2,1,0:T(8,128)(2,1)S(1)} %slice.119), channel_id=1, source_target_pairs={{0,2},{1,3},{2,0},{3,1},{4,6},{5,7},{6,4},{7,5},{8,10},{9,11},{10,... | collective-permute-start | bytes 491528 | tf_op jit(solution)/shard_map/ppermute | solution.py:214
  127.6 11.5 %collective-permute-done.7 = bf16[2,4,80,128]{3,2,1,0:T(8,128)(2,1)S(1)} collective-permute-done((bf16[2,4,80,128]{3,2,1,0:T(8,128)(2,1)S(1)}, bf16[2,4,80,128]{3,2,1,0:T(8,128)(2,1)S(1)}, u32[]{:S(2)}, u32[]{:S(2)}) %collective-permute-start.7) | collective-permute-done | bytes 163872 | tf_op jit(solution)/shard_map/ppermute | solution.py:214
  139.2 1.5 collective-permute-start.8
  140.8 2.9 %collective-permute-done.8 = bf16[1,4,80,128]{3,2,1,0:T(8,128)(2,1)S(1)} collective-permute-done((bf16[1,4,80,128]{3,2,1,0:T(8,128)(2,1)S(1)}, bf16[1,4,80,128]{3,2,1,0:T(8,128)(2,1)S(1)}, u32[]{:S(2)}, u32[]{:S(2)}) %collective-permute-start.8) | collective-permute-done | bytes 81952 | tf_op jit(solution)/shard_map/ppermute | solution.py:214
  144.5 1.9 %collective-permute-start.11 = (bf16[2,80,128]{2,1,0:T(8,128)(2,1)S(1)}, bf16[2,80,128]{2,1,0:T(8,128)(2,1)S(1)}, u32[]{:S(2)}, u32[]{:S(2)}) collective-permute-start(bf16[2,80,128]{2,1,0:T(8,128)(2,1)S(1)} %get-tuple-element.36), channel_id=1, source_target_pairs={{0,24},{8,16},{16,8},{24,0},{1,25},{9,17},{17,9},{25,1},{2,26},{10... | collective-permute-start | bytes 122888 | tf_op jit(solution)/shard_map/ppermute | solution.py:214
  147.9 2.4 %collective-permute-done.11 = bf16[2,80,128]{2,1,0:T(8,128)(2,1)S(1)} collective-permute-done((bf16[2,80,128]{2,1,0:T(8,128)(2,1)S(1)}, bf16[2,80,128]{2,1,0:T(8,128)(2,1)S(1)}, u32[]{:S(2)}, u32[]{:S(2)}) %collective-permute-start.11) | collective-permute-done | bytes 40992 | tf_op jit(solution)/shard_map/ppermute | solution.py:214
  151.4 1.6 collective-permute-start.12
  152.9 2.6 %all-to-all-start.2 = ((bf16[32,64,256]{2,1,0:T(8,128)(2,1)}), bf16[32,64,256]{2,1,0:T(8,128)(2,1)S(1)}, u32[]{:S(2)}, u32[]{:S(2)}) async-start(bf16[32,64,256]{2,1,0:T(8,128)(2,1)} %bitcast.29), calls=%async_computation.2 | async-start | bytes 2097152 | tf_op jit(solution)/shard_map/all_to_all | solution.py:204
  155.6 1.8 collective-permute-start.13
  157.4 9.7 %collective-permute-done.13 = bf16[2,2,80,128]{3,2,1,0:T(8,128)(2,1)S(1)} collective-permute-done((bf16[2,2,80,128]{3,2,1,0:T(8,128)(2,1)S(1)}, bf16[2,2,80,128]{3,2,1,0:T(8,128)(2,1)S(1)}, u32[]{:S(2)}, u32[]{:S(2)}) %collective-permute-start.13) | collective-permute-done | bytes 81952 | tf_op jit(solution)/shard_map/ppermute | solution.py:214
  167.3 1.4 collective-permute-done.14
  170.7 11.1 %all-to-all-done.2 = bf16[32,64,256]{2,1,0:T(8,128)(2,1)S(1)} async-done(((bf16[32,64,256]{2,1,0:T(8,128)(2,1)}), bf16[32,64,256]{2,1,0:T(8,128)(2,1)S(1)}, u32[]{:S(2)}, u32[]{:S(2)}) %all-to-all-start.2) | async-done | bytes 1048608 | tf_op jit(solution)/shard_map/all_to_all | solution.py:204
  182.7 8.4 %update_table.1 = f32[4096,256]{1,0:T(8,128)} custom-call(s32[1,2048]{1,0:T(1,128)} %get-tuple-element.14.request_ref, s32[4,8,128]{2,1,0:T(8,128)} %bitcast.143, bf16[2048,256]{1,0:T(8,128)(2,1)} %bitcast.134, f32[4096,256]{1,0:T(8,128)} %table_ref.3), custom_call_target="tpu_custom_call" | custom-call | tf_op jit(solution)/shard_map/update_table/pallas_call | solution.py:186
  (63 shorter events, 11.5 us)
Async XLA Ops:
  0.6 1.0 copy-start
  1.6 5.7 %collective-permute-start.2 = (bf16[16,1280]{1,0:T(8,128)(2,1)S(1)}, bf16[16,1280]{1,0:T(8,128)(2,1)S(1)}, u32[]{:S(2)}, u32[]{:S(2)}) collective-permute-start(bf16[16,1280]{1,0:T(8,128)(2,1)S(1)} %pad_maximum_fusion.5), channel_id=1, source_target_pairs={{0,8},{8,0},{16,24},{24,16},{1,9},{9,1},{17,25},{25,17},{2,10},{10... | collective-permute-start | bytes 122888 | tf_op jit(solution)/shard_map/ppermute | solution.py:214
  4.7 5.7 %collective-permute-start.1 = (bf16[16,1280]{1,0:T(8,128)(2,1)S(1)}, bf16[16,1280]{1,0:T(8,128)(2,1)S(1)}, u32[]{:S(2)}, u32[]{:S(2)}) collective-permute-start(bf16[16,1280]{1,0:T(8,128)(2,1)S(1)} %pad_maximum_fusion.5), channel_id=1, source_target_pairs={{0,16},{8,24},{16,0},{24,8},{1,17},{9,25},{17,1},{25,9},{2,18},{10... | collective-permute-start | bytes 122888 | tf_op jit(solution)/shard_map/ppermute | solution.py:214
  7.3 5.8 %collective-permute-start = (bf16[16,1280]{1,0:T(8,128)(2,1)S(1)}, bf16[16,1280]{1,0:T(8,128)(2,1)S(1)}, u32[]{:S(2)}, u32[]{:S(2)}) collective-permute-start(bf16[16,1280]{1,0:T(8,128)(2,1)S(1)} %pad_maximum_fusion.5), channel_id=1, source_target_pairs={{0,24},{8,16},{16,8},{24,0},{1,25},{9,17},{17,9},{25,1},{2,26},{10... | collective-permute-start | bytes 122888 | tf_op jit(solution)/shard_map/ppermute | solution.py:214
  13.2 5.4 %collective-permute-start.3 = (bf16[1,4,16,1280]{3,2,1,0:T(8,128)(2,1)S(1)}, bf16[1,4,16,1280]{3,2,1,0:T(8,128)(2,1)S(1)}, u32[]{:S(2)}, u32[]{:S(2)}) collective-permute-start(bf16[1,4,16,1280]{3,2,1,0:T(8,128)(2,1)S(1)} %maximum_bitcast_fusion.1), channel_id=1, source_target_pairs={{0,4},{1,5},{2,6},{3,7},{4,0},{5,1},{6,2},{7,3},{8,12},{9,13},{10,... | collective-permute-start | bytes 491528 | tf_op jit(solution)/shard_map/ppermute | solution.py:214
  18.7 24.7 %collective-permute-start.4 = (bf16[2,4,16,1280]{3,2,1,0:T(8,128)(2,1)S(1)}, bf16[2,4,16,1280]{3,2,1,0:T(8,128)(2,1)}, u32[]{:S(2)}, u32[]{:S(2)}) collective-permute-start(bf16[2,4,16,1280]{3,2,1,0:T(8,128)(2,1)S(1)} %maximum_bitcast_fusion), channel_id=1, source_target_pairs={{0,2},{1,3},{2,0},{3,1},{4,6},{5,7},{6,4},{7,5},{8,10},{9,11},{10,... | collective-permute-start | bytes 983048 | tf_op jit(solution)/shard_map/ppermute | solution.py:214
  21.9 9.7 %all-to-all-start = ((s32[32,1,64]{2,1,0:T(1,128)}), s32[32,1,64]{2,1,0:T(1,128)S(1)}, u32[]{:S(2)}, u32[]{:S(2)}) async-start(s32[32,1,64]{2,1,0:T(1,128)} %bitcast.144), calls=%async_computation | async-start | bytes 32768 | tf_op jit(solution)/shard_map/all_to_all | solution.py:204
  31.6 0.6 copy-start.4
  40.6 28.8 %all-to-all-start.1 = ((bf16[32,64,256]{2,1,0:T(8,128)(2,1)}), bf16[32,64,256]{2,1,0:T(8,128)(2,1)S(1)}, u32[]{:S(2)}, u32[]{:S(2)}) async-start(bf16[32,64,256]{2,1,0:T(8,128)(2,1)} %bitcast.139), calls=%async_computation.1 | async-start | bytes 2097152 | tf_op jit(solution)/shard_map/all_to_all | solution.py:204
  44.5 2.2 %collective-permute-start.5 = (bf16[4,4,16,1280]{3,2,1,0:T(8,128)(2,1)S(1)}, bf16[4,4,16,1280]{3,2,1,0:T(8,128)(2,1)S(1)}, u32[]{:S(2)}, u32[]{:S(2)}) collective-permute-start(bf16[4,4,16,1280]{3,2,1,0:T(8,128)(2,1)S(1)} %bitcast.135), channel_id=1, source_target_pairs={{0,1},{1,0},{2,3},{3,2},{4,5},{5,4},{6,7},{7,6},{8,9},{9,8},{10,11... | collective-permute-start | bytes 1966088 | tf_op jit(solution)/shard_map/ppermute | solution.py:214
  69.4 1.0 copy-start.1
  120.5 4.9 %copy-start.3 = (bf16[8,4,80,128]{3,2,1,0:T(8,128)(2,1)S(1)}, bf16[8,4,80,128]{3,2,1,0:T(8,128)(2,1)}, u32[]{:S(2)}) copy-start(bf16[8,4,80,128]{3,2,1,0:T(8,128)(2,1)} %get-tuple-element.21) | copy-start | bytes 1966084
  121.6 3.9 %collective-permute-start.6 = (bf16[4,4,80,128]{3,2,1,0:T(8,128)(2,1)S(1)}, bf16[4,4,80,128]{3,2,1,0:T(8,128)(2,1)S(1)}, u32[]{:S(2)}, u32[]{:S(2)}) collective-permute-start(bf16[4,4,80,128]{3,2,1,0:T(8,128)(2,1)S(1)} %slice.51), channel_id=1, source_target_pairs={{0,1},{1,0},{2,3},{3,2},{4,5},{5,4},{6,7},{7,6},{8,9},{9,8},{10,11... | collective-permute-start | bytes 983048 | tf_op jit(solution)/shard_map/ppermute | solution.py:214
  121.7 19.1 %all-to-all-start.3 = ((bf16[8,4,80,128]{3,2,1,0:T(8,128)(2,1)}), bf16[8,4,80,128]{3,2,1,0:T(8,128)(2,1)S(1)}, u32[]{:S(2)}, u32[]{:S(2)}) async-start(bf16[8,4,80,128]{3,2,1,0:T(8,128)(2,1)} %get-tuple-element.22), calls=%async_computation.3 | async-start | bytes 1310720 | tf_op jit(solution)/shard_map/all_to_all | solution.py:204
  125.6 13.6 %collective-permute-start.7 = (bf16[2,4,80,128]{3,2,1,0:T(8,128)(2,1)S(1)}, bf16[2,4,80,128]{3,2,1,0:T(8,128)(2,1)S(1)}, u32[]{:S(2)}, u32[]{:S(2)}) collective-permute-start(bf16[2,4,80,128]{3,2,1,0:T(8,128)(2,1)S(1)} %slice.119), channel_id=1, source_target_pairs={{0,2},{1,3},{2,0},{3,1},{4,6},{5,7},{6,4},{7,5},{8,10},{9,11},{10,... | collective-permute-start | bytes 491528 | tf_op jit(solution)/shard_map/ppermute | solution.py:214
  139.2 4.5 %collective-permute-start.8 = (bf16[1,4,80,128]{3,2,1,0:T(8,128)(2,1)S(1)}, bf16[1,4,80,128]{3,2,1,0:T(8,128)(2,1)S(1)}, u32[]{:S(2)}, u32[]{:S(2)}) collective-permute-start(bf16[1,4,80,128]{3,2,1,0:T(8,128)(2,1)S(1)} %slice.120), channel_id=1, source_target_pairs={{0,4},{1,5},{2,6},{3,7},{4,0},{5,1},{6,2},{7,3},{8,12},{9,13},{10,... | collective-permute-start | bytes 245768 | tf_op jit(solution)/shard_map/ppermute | solution.py:214
  143.8 4.1 %collective-permute-start.9 = (bf16[2,80,128]{2,1,0:T(8,128)(2,1)S(1)}, bf16[2,80,128]{2,1,0:T(8,128)(2,1)S(1)}, u32[]{:S(2)}, u32[]{:S(2)}) collective-permute-start(bf16[2,80,128]{2,1,0:T(8,128)(2,1)S(1)} %get-tuple-element.35), channel_id=1, source_target_pairs={{0,8},{8,0},{16,24},{24,16},{1,9},{9,1},{17,25},{25,17},{2,10},{10... | collective-permute-start | bytes 122888 | tf_op jit(solution)/shard_map/ppermute | solution.py:214
  144.5 5.8 %collective-permute-start.11 = (bf16[2,80,128]{2,1,0:T(8,128)(2,1)S(1)}, bf16[2,80,128]{2,1,0:T(8,128)(2,1)S(1)}, u32[]{:S(2)}, u32[]{:S(2)}) collective-permute-start(bf16[2,80,128]{2,1,0:T(8,128)(2,1)S(1)} %get-tuple-element.36), channel_id=1, source_target_pairs={{0,24},{8,16},{16,8},{24,0},{1,25},{9,17},{17,9},{25,1},{2,26},{10... | collective-permute-start | bytes 122888 | tf_op jit(solution)/shard_map/ppermute | solution.py:214
  146.4 4.9 %collective-permute-start.10 = (bf16[2,80,128]{2,1,0:T(8,128)(2,1)S(1)}, bf16[2,80,128]{2,1,0:T(8,128)(2,1)S(1)}, u32[]{:S(2)}, u32[]{:S(2)}) collective-permute-start(bf16[2,80,128]{2,1,0:T(8,128)(2,1)S(1)} %get-tuple-element.37), channel_id=1, source_target_pairs={{0,16},{8,24},{16,0},{24,8},{1,17},{9,25},{17,1},{25,9},{2,18},{10... | collective-permute-start | bytes 122888 | tf_op jit(solution)/shard_map/ppermute | solution.py:214
  151.4 4.2 %collective-permute-start.12 = (bf16[1,2,80,128]{3,2,1,0:T(8,128)(2,1)S(1)}, bf16[1,2,80,128]{3,2,1,0:T(8,128)(2,1)S(1)}, u32[]{:S(2)}, u32[]{:S(2)}) collective-permute-start(bf16[1,2,80,128]{3,2,1,0:T(8,128)(2,1)S(1)} %fusion.9), channel_id=1, source_target_pairs={{0,4},{1,5},{2,6},{3,7},{4,0},{5,1},{6,2},{7,3},{8,12},{9,13},{10,... | collective-permute-start | bytes 122888 | tf_op jit(solution)/shard_map/ppermute | solution.py:214
  152.9 28.8 %all-to-all-start.2 = ((bf16[32,64,256]{2,1,0:T(8,128)(2,1)}), bf16[32,64,256]{2,1,0:T(8,128)(2,1)S(1)}, u32[]{:S(2)}, u32[]{:S(2)}) async-start(bf16[32,64,256]{2,1,0:T(8,128)(2,1)} %bitcast.29), calls=%async_computation.2 | async-start | bytes 2097152 | tf_op jit(solution)/shard_map/all_to_all | solution.py:204
  155.6 11.5 %collective-permute-start.13 = (bf16[2,2,80,128]{3,2,1,0:T(8,128)(2,1)S(1)}, bf16[2,2,80,128]{3,2,1,0:T(8,128)(2,1)S(1)}, u32[]{:S(2)}, u32[]{:S(2)}) collective-permute-start(bf16[2,2,80,128]{3,2,1,0:T(8,128)(2,1)S(1)} %maximum_bitcast_fusion.2), channel_id=1, source_target_pairs={{0,2},{1,3},{2,0},{3,1},{4,6},{5,7},{6,4},{7,5},{8,10},{9,11},{10,... | collective-permute-start | bytes 245768 | tf_op jit(solution)/shard_map/ppermute | solution.py:214
  167.2 1.5 collective-permute-start.14
  181.8 1.0 copy-start.2
